TPU v7x, 256 devices: a whole 4x4x8 slice. The times are simulated.
256 devices in a mesh: ia: 8 (over z_lo, core), ja: 32 (over y, x, z_hi).
Axes of the slice: x: 4, y: 4, z: 8 (z_hi: 2, z_lo: 4; z = z_hi * 4 + z_lo), core: 2. Of those that a mesh axis runs over, the one named last changes fastest.
Arguments:
- slab_rows: bfloat16 [256, 768, 128], P('ia', 'ja'), may hold values from -6 to 6
- column_rows: bfloat16 [512, 768, 128], P('ja', 'ia'), may hold values from -6 to 6
- pair_tile: bfloat16 [256, 512, 128], P('ia', 'ja'), may hold values from -6 to 6
- cotangent: bfloat16 [256, 512, 128], P('ia', 'ja'), may hold values from -6 to 6
- weights_left: bfloat16 [128, 256], replicated, may hold values from -0.5 to 0.5
- weights_right: bfloat16 [128, 256], replicated, may hold values from -0.5 to 0.5
- gate_weight: bfloat16 [128, 128], replicated, may hold values from -0.5 to 0.5
- out_weight: bfloat16 [128, 128], replicated, may hold values from -0.5 to 0.5
- input_gain: float32 [128], replicated, may hold values from 0.1 to 1.9
- input_bias: float32 [128], replicated, may hold values from -3 to 3
- update_gain: float32 [128], replicated, may hold values from 0.1 to 1.9
- update_bias: float32 [128], replicated, may hold values from -3 to 3
Outputs:
- update: bfloat16 [256, 512, 128], P('ia', 'ja')
- grad_slab: bfloat16 [256, 768, 128], P('ia', 'ja')
- grad_columns: bfloat16 [512, 768, 128], P('ja', 'ia')
- grad_tile: bfloat16 [256, 512, 128], P('ia', 'ja')
All inputs are finite; a program needn't handle non-finite values.
Results may differ from a plain program's by a relative error of at most 0.018.
Values may be sent and summed in bfloat16 or wider, within the bound.
No kernel may reach another device: no remote copies, remote signals or barrier semaphores. Data moves between devices by JAX's collectives and lax.ppermute only.
A program may use at most 128 MiB of HBM per device.

v0:
```python
import jax
import jax.numpy as jnp
from jax import lax
from jax.sharding import Mesh
from jax.sharding import PartitionSpec as P

JA = ("ja_0", "ja_1", "ja_2")


epsilon = 1e-05


def summed_rows(terms, axes):
    total = terms.astype(jnp.bfloat16)
    for axis in axes:
        total = lax.psum_scatter(total, axis, scatter_dimension=0, tiled=True)
    return total.astype(jnp.float32)


def in_blocks(array, dim, devices):
    before, after = (array.shape[:dim], array.shape[dim + 1 :])
    return jnp.moveaxis(array.reshape(*before, devices, -1, *after), dim, 0)


def sent_and_summed(array, axis, dim):
    devices = lax.axis_size(axis)
    blocks = lax.all_to_all(in_blocks(array, dim, devices), axis, 0, 0, tiled=True)
    return jnp.sum(blocks.astype(jnp.float32), axis=0)


def normalize(values, gain, bias):
    values = values.astype(jnp.float32)
    centre = jnp.mean(values, axis=-1, keepdims=True)
    shifted = values - centre
    inverse = lax.rsqrt(jnp.mean(shifted * shifted, axis=-1, keepdims=True) + epsilon)
    scaled = shifted * inverse
    return (scaled * gain + bias, scaled, inverse)


def norm_back(scaled, inverse, grad_out, gain):
    grad_hat = grad_out * gain
    first_mean = jnp.mean(grad_hat, axis=-1, keepdims=True)
    second_mean = jnp.mean(grad_hat * scaled, axis=-1, keepdims=True)
    return inverse * (grad_hat - first_mean - scaled * second_mean)


def project(rows, weights, input_gain, input_bias):
    normed, scaled, inverse = normalize(rows, input_gain, input_bias)
    hidden = jnp.dot(normed.astype(jnp.bfloat16), weights, preferred_element_type=jnp.float32)
    half_width = weights.shape[1] // 2
    linear = hidden[..., :half_width]
    sigma = jax.nn.sigmoid(hidden[..., half_width:])
    return ((sigma * linear).astype(jnp.bfloat16), linear, sigma, scaled, inverse)


def project_back(grad_edge, linear, sigma, scaled, inverse, weights, input_gain):
    joined = jnp.concatenate(
        [grad_edge * sigma, grad_edge * linear * sigma * (1.0 - sigma)], axis=-1
    )
    grad_norm = jnp.dot(joined.astype(jnp.bfloat16), weights.T, preferred_element_type=jnp.float32)
    return norm_back(scaled, inverse, grad_norm, input_gain).astype(jnp.bfloat16)


def shards(
    slab_rows,
    column_rows,
    pair_tile,
    cotangent,
    weights_left,
    weights_right,
    gate_weight,
    out_weight,
    input_gain,
    input_bias,
    update_gain,
    update_bias,
):
    left, lin_left, sig_left, scaled_left, inv_left = project(
        slab_rows, weights_left, input_gain, input_bias
    )
    right, lin_right, sig_right, scaled_right, inv_right = project(
        column_rows, weights_right, input_gain, input_bias
    )
    left_whole = lax.all_gather(left, JA, axis=1, tiled=True)
    panel_piece = lax.all_gather(right, "ia", axis=1, tiled=True)
    left_slice = left_whole
    running = jnp.einsum(
        "ikc,jkc->ijc", left_slice, panel_piece, preferred_element_type=jnp.float32
    )
    tri_norm, tri_scaled, tri_inverse = normalize(running, update_gain, update_bias)
    outer = jnp.dot(tri_norm.astype(jnp.bfloat16), out_weight, preferred_element_type=jnp.float32)
    tile_norm, tile_scaled, tile_inverse = normalize(pair_tile, input_gain, input_bias)
    gate_linear = jnp.dot(
        tile_norm.astype(jnp.bfloat16), gate_weight, preferred_element_type=jnp.float32
    )
    gate = jax.nn.sigmoid(gate_linear)
    update = (gate * outer).astype(jnp.bfloat16)
    grad_update = cotangent.astype(jnp.float32)
    grad_outer = (grad_update * gate).astype(jnp.bfloat16)
    grad_gate = (grad_update * outer * gate * (1.0 - gate)).astype(jnp.bfloat16)
    grad_tnorm = jnp.dot(grad_outer, out_weight.T, preferred_element_type=jnp.float32)
    grad_tri = norm_back(tri_scaled, tri_inverse, grad_tnorm, update_gain).astype(jnp.bfloat16)
    grad_pnorm = jnp.dot(grad_gate, gate_weight.T, preferred_element_type=jnp.float32)
    grad_tile = norm_back(tile_scaled, tile_inverse, grad_pnorm, input_gain).astype(jnp.bfloat16)
    left_sums = summed_rows(
        jnp.einsum("ijc,jkc->kic", grad_tri, panel_piece, preferred_element_type=jnp.float32), JA
    )
    left_slice = left_whole
    right_sums = sent_and_summed(
        jnp.einsum("ijc,ikc->kjc", grad_tri, left_slice, preferred_element_type=jnp.float32).astype(
            jnp.bfloat16
        ),
        "ia",
        0,
    )
    grad_left = jnp.transpose(left_sums, (1, 0, 2))
    grad_right = jnp.transpose(right_sums, (1, 0, 2))
    grad_slab = project_back(
        grad_left, lin_left, sig_left, scaled_left, inv_left, weights_left, input_gain
    )
    grad_columns = project_back(
        grad_right, lin_right, sig_right, scaled_right, inv_right, weights_right, input_gain
    )
    return (update, grad_slab, grad_columns, grad_tile)


def solution(mesh):
    finer = Mesh(mesh.devices.reshape(mesh.shape["ia"], 4, 4, 2), ("ia", "ja_0", "ja_1", "ja_2"))
    in_specs = (
        P("ia", JA, None),
        P(JA, "ia", None),
        P("ia", JA, None),
        P("ia", JA, None),
        P(),
        P(),
        P(),
        P(),
        P(),
        P(),
        P(),
        P(),
    )
    out_specs = (P("ia", JA, None), P("ia", JA, None), P(JA, "ia", None), P("ia", JA, None))
    return jax.shard_map(
        shards, mesh=finer, in_specs=in_specs, out_specs=out_specs, check_vma=False
    )
```

profile of v0, /device:TPU:1, one launch (start us, length us, event | category | flops | bytes accessed | tf_op | source)
XLA Modules:
  0.0 401.9 jit_solution(11439921015196536878)
XLA Ops:
  7.3 1.3 convert_reduce_fusion.1
  8.6 1.6 fusion.14
  10.2 1.6 fusion.37
  11.9 1.1 copy-done.1
  13.0 1.0 multiply_convert_fusion.1
  14.0 0.2 convert_reduce_fusion.2
  14.2 0.3 fusion.36
  14.6 0.4 fusion.69
  15.0 0.9 copy-done.5
  15.9 0.8 multiply_convert_fusion.2
  16.8 0.2 reduce-scatter.6.cloned.1.call-start
  17.0 0.1 convert_reduce_fusion.3
  17.3 0.2 fusion.64
  17.7 0.6 copy-done.17
  18.3 0.3 fusion.2
  18.7 0.7 copy-done.9
  19.4 0.2 fusion.76
  19.6 1.4 copy.77
  21.0 39.5 %all-gather.3.cloned.1.call-done = bf16[16,768,128]{2,1,0:T(8,128)(2,1)} async-done(((bf16[16,96,128]{2,1,0:T(8,128)(2,1)}), bf16[16,768,128]{2,1,0:T(8,128)(2,1)}) %all-gather.3.cloned.1.call-update) | async-done | bytes 3145744 | tf_op jit(solution)/shard_map/all_gather | solution.py:85
  60.6 3.9 copy.74
  64.5 137.4 %all-gather.5.cloned.1.call-done = bf16[32,768,128]{2,1,0:T(8,128)(2,1)} async-done(((bf16[32,24,128]{2,1,0:T(8,128)(2,1)}), bf16[32,768,128]{2,1,0:T(8,128)(2,1)}) %all-gather.5.cloned.1.call-update) | async-done | bytes 6291472 | tf_op jit(solution)/shard_map/all_gather | solution.py:84
  201.9 41.8 %copy.75 = bf16[32,768,128]{0,1,2:T(8,128)(2,1)} copy(bf16[32,768,128]{2,1,0:T(8,128)(2,1)} %all-gather.5.cloned.1.call-done) | data formatting | bytes 12582912 | tf_op jit(solution)/shard_map/all_gather | solution.py:84
  243.7 10.1 %fusion.99 = (f32[32,16]{0,1:T(8,128)S(1)}, f32[32,16,128]{0,1,2:T(8,128)S(1)}) fusion(bf16[16,768,128]{1,0,2:T(8,128)(2,1)S(1)} %copy.74, bf16[32,768,128]{0,1,2:T(8,128)(2,1)} %copy.75), kind=kOutput, calls=%fused_computation.142 | convolution fusion | flops 100728320 | bytes 9701376 | tf_op jit(solution)/shard_map/ikc,jkc->ijc/dot_general | solution.py:87
  253.9 0.2 multiply_reduce_fusion.1
  254.1 0.3 multiply_reduce_fusion.2
  254.5 1.3 multiply_convert_fusion
  255.8 0.8 copy-done.4
  256.6 4.6 %convert_bitcast_fusion = bf16[768,32,128]{0,1,2:T(8,128)(2,1)} fusion(bf16[16,768,128]{1,0,2:T(8,128)(2,1)S(1)} %copy.74, bf16[32,16,128]{0,1,2:T(8,128)(2,1)S(1)} %get-tuple-element.14), kind=kOutput, calls=%fused_computation.1 | convolution fusion | flops 103809024 | bytes 9568256 | tf_op jit(solution)/shard_map/ijc,jkc->kic/dot_general | solution.py:106
  261.1 9.6 %copy.79 = bf16[768,32,128]{2,1,0:T(8,128)(2,1)} copy(bf16[768,32,128]{0,1,2:T(8,128)(2,1)} %convert_bitcast_fusion) | data formatting | bytes 12582912 | tf_op jit(solution)/shard_map/convert_element_type | solution.py:14
  270.7 14.0 %convert_bitcast_fusion.1 = bf16[768,16,128]{0,1,2:T(8,128)(2,1)S(1)} fusion(bf16[32,768,128]{0,1,2:T(8,128)(2,1)} %copy.75, bf16[32,16,128]{0,1,2:T(8,128)(2,1)} %copy-done.4), kind=kOutput, calls=%fused_computation.2 | convolution fusion | flops 102236160 | bytes 9568256 | tf_op jit(solution)/shard_map/ijc,ikc->kjc/dot_general | solution.py:110
  284.7 4.0 copy.82
  288.7 6.5 %all-to-all-start = ((bf16[8,96,16,128]{3,2,1,0:T(8,128)(2,1)}), bf16[8,96,16,128]{3,2,1,0:T(8,128)(2,1)}, u32[]{:S(2)}, u32[]{:S(2)}) async-start(bf16[8,96,16,128]{3,2,1,0:T(8,128)(2,1)} %bitcast.75), calls=%async_computation.2 | async-start | bytes 6291456 | tf_op jit(solution)/shard_map/all_to_all | solution.py:27
  295.2 37.4 %reduce-scatter.6.cloned.1.call-done = bf16[192,32,128]{2,1,0:T(8,128)(2,1)} async-done(((bf16[768,32,128]{2,1,0:T(8,128)(2,1)}), bf16[192,32,128]{2,1,0:T(8,128)(2,1)}) %reduce-scatter.6.cloned.1.call-update) | async-done | bytes 1572880 | tf_op jit(solution)/shard_map/reduce_scatter | solution.py:16
  332.6 0.3 reduce-scatter.10.cloned.1.call-start
  332.9 0.5 copy.76
  333.4 0.8 multiply_convert_fusion.3
  334.3 0.4 fusion.98
  335.0 1.0 fusion.63
  336.0 29.9 %all-to-all-done = bf16[8,96,16,128]{3,2,1,0:T(8,128)(2,1)} async-done(((bf16[8,96,16,128]{3,2,1,0:T(8,128)(2,1)}), bf16[8,96,16,128]{3,2,1,0:T(8,128)(2,1)}, u32[]{:S(2)}, u32[]{:S(2)}) %all-to-all-start) | async-done | bytes 3145760 | tf_op jit(solution)/shard_map/all_to_all | solution.py:27
  365.9 2.4 convert_reduce_fusion
  368.4 1.1 fusion.21
  369.5 2.0 copy.97
  371.6 2.1 fusion.96
  373.6 1.7 fusion.13
  375.3 17.2 %reduce-scatter.10.cloned.1.call-done = bf16[24,4096]{1,0:T(8,128)(2,1)} async-done(((bf16[48,4096]{1,0:T(8,128)(2,1)}), bf16[24,4096]{1,0:T(8,128)(2,1)}) %reduce-scatter.10.cloned.1.call-update) | async-done | bytes 196624
  392.5 1.1 fusion.45
  393.7 0.5 fusion.97
  394.2 1.2 fusion.35
  (101 shorter events, 1.1 us)
Async XLA Ops:
  7.2 3.0 copy-start
  7.2 7.4 %copy-start.31 = (f32[128]{0:T(128)S(1)}, f32[128]{0:T(128)}, u32[]{:S(2)}) copy-start(f32[128]{0:T(128)} %param.20) | copy-start | bytes 1540
  7.2 7.4 %copy-start.34 = (f32[128]{0:T(128)S(1)}, f32[128]{0:T(128)}, u32[]{:S(2)}) copy-start(f32[128]{0:T(128)} %param.21) | copy-start | bytes 1540
  7.2 6.8 %copy-start.8 = (bf16[32,24,128]{2,1,0:T(8,128)(2,1)S(1)}, bf16[32,24,128]{2,1,0:T(8,128)(2,1)}, u32[]{:S(2)}) copy-start(bf16[32,24,128]{2,1,0:T(8,128)(2,1)} %param.12) | copy-start | bytes 589828
  7.2 7.4 %copy-start.27 = (bf16[128,256]{1,0:T(8,128)(2,1)S(1)}, bf16[128,256]{1,0:T(8,128)(2,1)}, u32[]{:S(2)}) copy-start(bf16[128,256]{1,0:T(8,128)(2,1)} %param.16) | copy-start | bytes 196612
  7.2 53.3 %all-gather.3.cloned.1.call-start = ((), (), s32[]{:S(2)}) async-start(), calls=%async_computation.4 | async-start | bytes 3538944 | tf_op jit(solution)/shard_map/all_gather | solution.py:85
  8.6 1.6 copy-start.21
  10.2 1.7 copy-start.25
  10.2 6.8 %copy-start.12 = (bf16[32,16,128]{2,1,0:T(8,128)(2,1)S(1)}, bf16[32,16,128]{2,1,0:T(8,128)(2,1)}, u32[]{:S(2)}) copy-start(bf16[32,16,128]{2,1,0:T(8,128)(2,1)} %param.14) | copy-start | bytes 393220
  11.9 1.1 copy-start.1
  13.0 5.3 %copy-start.29 = (bf16[128,128]{1,0:T(8,128)(2,1)S(1)}, bf16[128,128]{1,0:T(8,128)(2,1)}, u32[]{:S(2)}) copy-start(bf16[128,128]{1,0:T(8,128)(2,1)} %param.18) | copy-start | bytes 98308
  13.0 6.4 %copy-start.13 = (bf16[32,16,128]{2,1,0:T(8,128)(2,1)S(1)}, bf16[32,16,128]{2,1,0:T(8,128)(2,1)}, u32[]{:S(2)}) copy-start(bf16[32,16,128]{2,1,0:T(8,128)(2,1)} %param.15) | copy-start | bytes 393220
  13.0 6.4 %copy-start.23 = (bf16[128,128]{1,0:T(8,128)(2,1)S(1)}, bf16[128,128]{1,0:T(8,128)(2,1)}, u32[]{:S(2)}) copy-start(bf16[128,128]{1,0:T(8,128)(2,1)} %param.19) | copy-start | bytes 98308
  14.0 187.9 %all-gather.5.cloned.1.call-start = ((), (), s32[]{:S(2)}) async-start(), calls=%async_computation.5 | async-start | bytes 6488064 | tf_op jit(solution)/shard_map/all_gather | solution.py:84
  14.2 6.8 %copy-start.15 = (f32[32,24]{1,0:T(8,128)}, f32[32,24]{1,0:T(8,128)S(1)}, u32[]{:S(2)}) copy-start(f32[32,24]{1,0:T(8,128)S(1)} %broadcast_multiply_fusion.2) | copy-start | bytes 9220
  14.6 6.4 %copy-start.19 = (f32[32,24]{1,0:T(8,128)}, f32[32,24]{1,0:T(8,128)S(1)}, u32[]{:S(2)}) copy-start(f32[32,24]{1,0:T(8,128)S(1)} %add_rsqrt_fusion) | copy-start | bytes 9220
  15.0 0.9 copy-start.5
  16.8 315.8 %reduce-scatter.6.cloned.1.call-start = ((), (), s32[]{:S(2)}) async-start(), calls=%async_computation.6 | async-start | bytes 7864320 | tf_op jit(solution)/shard_map/reduce_scatter | solution.py:16
  17.7 0.6 copy-start.17
  18.7 0.7 copy-start.9
  243.7 10.4 %copy-start.3 = (f32[32,16,128]{0,1,2:T(8,128)S(1)}, f32[32,16,128]{0,1,2:T(8,128)}, u32[]{:S(2)}) copy-start(f32[32,16,128]{0,1,2:T(8,128)} %copy.77) | copy-start | bytes 786436
  243.7 10.4 %copy-start.35 = (f32[128]{0:T(128)S(1)}, f32[128]{0:T(128)}, u32[]{:S(2)}) copy-start(f32[128]{0:T(128)} %param.22) | copy-start | bytes 1540
  253.9 0.7 copy-start.36
  255.8 0.8 copy-start.4
  288.7 44.2 %copy-start.11 = (bf16[32,16,128]{0,1,2:T(8,128)(2,1)S(1)}, bf16[32,16,128]{0,1,2:T(8,128)(2,1)}, u32[]{:S(2)}) copy-start(bf16[32,16,128]{0,1,2:T(8,128)(2,1)} %get-tuple-element.15) | copy-start | bytes 393220
  288.7 44.8 %copy-start.10 = (f32[32,16,128]{2,1,0:T(8,128)S(1)}, f32[32,16,128]{2,1,0:T(8,128)}, u32[]{:S(2)}) copy-start(f32[32,16,128]{2,1,0:T(8,128)} %copy-done.9) | copy-start | bytes 786436
  288.7 44.8 %copy-start.24 = (bf16[128,128]{1,0:T(8,128)(2,1)S(1)}, bf16[128,128]{1,0:T(8,128)(2,1)}, u32[]{:S(2)}) copy-start(bf16[128,128]{1,0:T(8,128)(2,1)} %param.19) | copy-start | bytes 98308
  288.7 45.6 %copy-start.14 = (bf16[32,16,128]{2,1,0:T(8,128)(2,1)S(1)}, bf16[32,16,128]{2,1,0:T(8,128)(2,1)}, u32[]{:S(2)}) copy-start(bf16[32,16,128]{2,1,0:T(8,128)(2,1)} %param.15) | copy-start | bytes 393220
  288.7 45.6 %copy-start.18 = (f32[32,16]{1,0:T(8,128)S(1)}, f32[32,16]{1,0:T(8,128)}, u32[]{:S(2)}) copy-start(f32[32,16]{1,0:T(8,128)} %copy-done.17) | copy-start | bytes 6148
  288.7 45.6 %copy-start.30 = (bf16[128,128]{1,0:T(8,128)(2,1)S(1)}, bf16[128,128]{1,0:T(8,128)(2,1)}, u32[]{:S(2)}) copy-start(bf16[128,128]{1,0:T(8,128)(2,1)} %param.18) | copy-start | bytes 98308
  288.7 45.6 %copy-start.32 = (f32[128]{0:T(128)S(1)}, f32[128]{0:T(128)}, u32[]{:S(2)}) copy-start(f32[128]{0:T(128)} %param.20) | copy-start | bytes 1540
  288.7 77.2 %all-to-all-start = ((bf16[8,96,16,128]{3,2,1,0:T(8,128)(2,1)}), bf16[8,96,16,128]{3,2,1,0:T(8,128)(2,1)}, u32[]{:S(2)}, u32[]{:S(2)}) async-start(bf16[8,96,16,128]{3,2,1,0:T(8,128)(2,1)} %bitcast.75), calls=%async_computation.2 | async-start | bytes 6291456 | tf_op jit(solution)/shard_map/all_to_all | solution.py:27
  295.2 74.3 %reduce-scatter.8.cloned.1.call-start = ((), (), s32[]{:S(2)}) async-start(), calls=%async_computation.7 | async-start | bytes 1966080 | tf_op jit(solution)/shard_map/reduce_scatter | solution.py:16
  332.6 59.9 %reduce-scatter.10.cloned.1.call-start = ((), (), s32[]{:S(2)}) async-start(), calls=%async_computation.8 | async-start | bytes 589824
  333.4 34.9 %copy-start.2 = (f32[16,96,256]{2,1,0:T(8,128)S(1)}, f32[16,96,256]{2,1,0:T(8,128)}, u32[]{:S(2)}) copy-start(f32[16,96,256]{2,1,0:T(8,128)} %copy-done.1) | copy-start | bytes 4718596
  368.3 3.2 copy-start.7
  368.3 3.2 copy-start.22
  368.3 3.2 copy-start.26
  368.3 3.2 copy-start.33
  369.5 23.0 %copy-start.6 = (f32[32,24,256]{2,1,0:T(8,128)S(1)}, f32[32,24,256]{2,1,0:T(8,128)}, u32[]{:S(2)}) copy-start(f32[32,24,256]{2,1,0:T(8,128)} %copy-done.5) | copy-start | bytes 2359300
  371.5 22.1 %copy-start.16 = (f32[32,24]{1,0:T(8,128)S(1)}, f32[32,24]{1,0:T(8,128)}, u32[]{:S(2)}) copy-start(f32[32,24]{1,0:T(8,128)} %copy-done.15) | copy-start | bytes 9220
  371.5 22.2 %copy-start.20 = (f32[32,24]{1,0:T(8,128)S(1)}, f32[32,24]{1,0:T(8,128)}, u32[]{:S(2)}) copy-start(f32[32,24]{1,0:T(8,128)} %copy-done.19) | copy-start | bytes 9220
  371.5 22.2 %copy-start.28 = (bf16[128,256]{1,0:T(8,128)(2,1)S(1)}, bf16[128,256]{1,0:T(8,128)(2,1)}, u32[]{:S(2)}) copy-start(bf16[128,256]{1,0:T(8,128)(2,1)} %param.16) | copy-start | bytes 196612
Sparse Core Ops, SparseCore 0:
  14.1 46.4 all-gather.2
  64.3 137.5 all-gather.4
  270.8 61.7 reduce-scatter.5
  335.0 27.1 reduce-scatter.7
  371.6 20.8 reduce-scatter.9
where the time goes:
time: 403 us; the launch traced here: 402 us
  waiting for transfers between devices  262 us (65%)
  local copies, waits for them, and re-layouts  68.1 us (17%)
  matrix products  35.1 us (9%)
  other arithmetic  15.8 us (4%)
  between operations  14.3 us (4%)
  starting transfers between devices  7.09 us (2%)
    all_gather x1, waiting for transfers between devices, shards(): left_whole = lax.all_gather(left, JA, axis=1, tiled=True)  137 us
    all_gather x1, local copies, waits for them, and re-layouts, shards(): left_whole = lax.all_gather(left, JA, axis=1, tiled=True)  41.8 us
    all_gather x1, waiting for transfers between devices, shards(): panel_piece = lax.all_gather(right, 'ia', axis=1, tiled=True)  39.5 us
    reduce_scatter x2, waiting for transfers between devices, summed_rows(): total = lax.psum_scatter(total, axis, scatter_dimension=0, tiled=True)  37.4 us
    all_to_all x1, waiting for transfers between devices, sent_and_summed(): lax.all_to_all(in_blocks(array, dim, devices), axis, 0, 0, tiled=True)  29.9 us
    unnamed x6, waiting for transfers between devices  17.3 us
    dot_general x1, matrix products, shards(): jnp.einsum('ijc,ikc->kjc', grad_tri, left_slice, preferred_element_type=j...  14 us
    dot_general x1, matrix products, shards(): jnp.einsum('ikc,jkc->ijc', left_slice, panel_piece, preferred_element_typ...  10.1 us
  transfers between devices with their start and end apart: 6, of which 5 were waited for; matrix products, arithmetic and copies ran while one was open for 9% of the time, Pallas kernels for 0%

commit v1 on v0

v1 whole, which is shorter than its diff:
```python
import jax
import jax.numpy as jnp
from jax import lax
from jax.sharding import Mesh
from jax.sharding import PartitionSpec as P

IA = ("zl", "co")
JA = ("y", "x", "zh")
SPLIT = ("zl", "y", "x", "zh")

epsilon = 1e-05


def normalize(values, gain, bias):
    values = values.astype(jnp.float32)
    centre = jnp.mean(values, axis=-1, keepdims=True)
    shifted = values - centre
    inverse = lax.rsqrt(jnp.mean(shifted * shifted, axis=-1, keepdims=True) + epsilon)
    scaled = shifted * inverse
    return (scaled * gain + bias, scaled, inverse)


def norm_back(scaled, inverse, grad_out, gain):
    grad_hat = grad_out * gain
    first_mean = jnp.mean(grad_hat, axis=-1, keepdims=True)
    second_mean = jnp.mean(grad_hat * scaled, axis=-1, keepdims=True)
    return inverse * (grad_hat - first_mean - scaled * second_mean)


def project(rows, weights, input_gain, input_bias):
    normed, scaled, inverse = normalize(rows, input_gain, input_bias)
    hidden = jnp.dot(normed.astype(jnp.bfloat16), weights, preferred_element_type=jnp.float32)
    half_width = weights.shape[1] // 2
    linear = hidden[..., :half_width]
    sigma = jax.nn.sigmoid(hidden[..., half_width:])
    return ((sigma * linear).astype(jnp.bfloat16), linear, sigma, scaled, inverse)


def project_back(grad_edge, linear, sigma, scaled, inverse, weights, input_gain):
    joined = jnp.concatenate(
        [grad_edge * sigma, grad_edge * linear * sigma * (1.0 - sigma)], axis=-1
    )
    grad_norm = jnp.dot(joined.astype(jnp.bfloat16), weights.T, preferred_element_type=jnp.float32)
    return norm_back(scaled, inverse, grad_norm, input_gain).astype(jnp.bfloat16)


def shuffled(array):
    return lax.all_to_all(array, SPLIT, 0, 0, tiled=True)


def swapped(array):
    return lax.ppermute(array, "co", [(0, 1), (1, 0)])


def dot32(spec, a, b):
    return jnp.einsum(spec, a, b, preferred_element_type=jnp.float32)


def shards(
    slab_rows,
    column_rows,
    pair_tile,
    cotangent,
    weights_left,
    weights_right,
    gate_weight,
    out_weight,
    input_gain,
    input_bias,
    update_gain,
    update_bias,
):
    core = lax.axis_index("co")
    left, lin_left, sig_left, scaled_left, inv_left = project(
        slab_rows, weights_left, input_gain, input_bias
    )
    right, lin_right, sig_right, scaled_right, inv_right = project(
        column_rows, weights_right, input_gain, input_bias
    )
    left_sent = jnp.transpose(left, (2, 1, 0)).reshape(128, 768)
    right_sent = jnp.transpose(right, (2, 0, 1)).reshape(128, 1536)
    got = shuffled(jnp.concatenate([left_sent, right_sent], axis=1))
    left_got = got[:, :768].reshape(4, 4, 2, 4, 24, 32)
    left_ki = jnp.transpose(left_got, (2, 1, 3, 4, 0, 5)).reshape(2, 384, 128)
    right_jk = jnp.transpose(got[:, 768:].reshape(4, 512, 96), (1, 0, 2)).reshape(512, 384)
    right_other = swapped(right_jk)
    left_own = jnp.where(core == 0, left_ki[0], left_ki[1])
    left_other = jnp.where(core == 0, left_ki[1], left_ki[0])
    tri = dot32("ki,jk->ij", left_own, right_jk) + dot32("ki,jk->ij", left_other, right_other)
    tri_sent = jnp.transpose(tri.astype(jnp.bfloat16).reshape(4, 32, 32, 16), (0, 2, 1, 3))
    tri_got = shuffled(tri_sent.reshape(128, 512))
    running = jnp.transpose(tri_got.astype(jnp.float32)).reshape(32, 16, 128)

    tri_norm, tri_scaled, tri_inverse = normalize(running, update_gain, update_bias)
    outer = jnp.dot(tri_norm.astype(jnp.bfloat16), out_weight, preferred_element_type=jnp.float32)
    tile_norm, tile_scaled, tile_inverse = normalize(pair_tile, input_gain, input_bias)
    gate_linear = jnp.dot(
        tile_norm.astype(jnp.bfloat16), gate_weight, preferred_element_type=jnp.float32
    )
    gate = jax.nn.sigmoid(gate_linear)
    update = (gate * outer).astype(jnp.bfloat16)
    grad_update = cotangent.astype(jnp.float32)
    grad_outer = (grad_update * gate).astype(jnp.bfloat16)
    grad_gate = (grad_update * outer * gate * (1.0 - gate)).astype(jnp.bfloat16)
    grad_tnorm = jnp.dot(grad_outer, out_weight.T, preferred_element_type=jnp.float32)
    grad_tri = norm_back(tri_scaled, tri_inverse, grad_tnorm, update_gain).astype(jnp.bfloat16)
    grad_pnorm = jnp.dot(grad_gate, gate_weight.T, preferred_element_type=jnp.float32)
    grad_tile = norm_back(tile_scaled, tile_inverse, grad_pnorm, input_gain).astype(jnp.bfloat16)

    d_got = shuffled(jnp.transpose(grad_tri.reshape(512, 128)))
    d_ij = jnp.transpose(d_got.reshape(4, 32, 32, 16), (0, 2, 1, 3)).reshape(128, 512)
    d_right_other = dot32("ij,ki->jk", d_ij, left_other).astype(jnp.bfloat16)
    d_right_come = swapped(d_right_other)
    d_left_own = dot32("jk,ij->ki", right_jk, d_ij)
    d_left_other = dot32("jk,ij->ki", right_other, d_ij)
    d_right = (dot32("ij,ki->jk", d_ij, left_own) + d_right_come.astype(jnp.float32)).astype(
        jnp.bfloat16
    )
    d_left = jnp.stack(
        [
            jnp.where(core == 0, d_left_own, d_left_other),
            jnp.where(core == 0, d_left_other, d_left_own),
        ]
    ).astype(jnp.bfloat16)
    d_left = jnp.transpose(d_left.reshape(2, 4, 4, 24, 4, 32), (4, 1, 0, 2, 3, 5)).reshape(128, 768)
    d_right = jnp.transpose(d_right.reshape(512, 4, 96), (1, 0, 2)).reshape(128, 1536)
    back = shuffled(jnp.concatenate([d_left, d_right], axis=1))
    grad_left = jnp.transpose(back[:, :768].reshape(128, 24, 32), (2, 1, 0)).astype(jnp.float32)
    grad_right = jnp.transpose(back[:, 768:].reshape(128, 16, 96), (1, 2, 0)).astype(jnp.float32)
    grad_slab = project_back(
        grad_left, lin_left, sig_left, scaled_left, inv_left, weights_left, input_gain
    )
    grad_columns = project_back(
        grad_right, lin_right, sig_right, scaled_right, inv_right, weights_right, input_gain
    )
    return (update, grad_slab, grad_columns, grad_tile)


def solution(mesh):
    finer = Mesh(mesh.devices.reshape(4, 2, 4, 4, 2), ("zl", "co", "y", "x", "zh"))
    row_spec = P(IA, JA, None)
    column_spec = P(JA, IA, None)
    in_specs = (row_spec, column_spec, row_spec, row_spec) + (P(),) * 8
    return jax.shard_map(
        shards,
        mesh=finer,
        in_specs=in_specs,
        out_specs=(row_spec, row_spec, column_spec, row_spec),
        check_vma=False,
    )
```

time: 403 us -> 188 us (0.47)
  waiting for transfers between devices: 262 us -> 46 us
  starting transfers between devices: 7.09 us -> 34.7 us
  local copies, waits for them, and re-layouts: 68.1 us -> 47.3 us
  matrix products: 35.1 us -> 16.1 us
  blocking collectives: 0 us -> 17.3 us
  between operations: 14.3 us -> 1.38 us
  other arithmetic: 15.8 us -> 23.5 us
    all_gather x2 -> x0, waiting for transfers between devices: 177 us -> none  [the longest x1 137 us: shards(): left_whole = lax.all_gather(left, JA, axis=1, tiled=True)]
    all_gather x2 -> x0, local copies, waits for them, and re-layouts: 45.7 us -> none  [the longest x1 41.8 us: shards(): left_whole = lax.all_gather(left, JA, axis=1, tiled=True)]
    reduce_scatter x2 -> x0, waiting for transfers between devices: 37.4 us -> none  [summed_rows(): total = lax.psum_scatter(total, axis, scatter_dimension=0, tiled=True)]
    all_to_all x1 -> x3, starting transfers between devices: 6.53 us -> 29.2 us  [shuffled(): return lax.all_to_all(array, SPLIT, 0, 0, tiled=True)]
    dot_general x3 -> x6, matrix products: 28.7 us -> 6.46 us  [dot32(): return jnp.einsum(spec, a, b, preferred_element_type=jnp.float32)]
    all_to_all x0 -> x1, blocking collectives: none -> 17.3 us  [shuffled(): return lax.all_to_all(array, SPLIT, 0, 0, tiled=True)]
    unnamed x6 -> x0, waiting for transfers between devices: 17.3 us -> none
    all_to_all x1 -> x3, waiting for transfers between devices: 29.9 us -> 46 us  [shuffled(): return lax.all_to_all(array, SPLIT, 0, 0, tiled=True)]
  transfers between devices with their start and end apart: 6 -> 5, of which waited for: 5 -> 3; matrix products, arithmetic and copies ran while one was open for 9% -> 11% of each run, Pallas kernels for 0% -> 0%
where the time goes in v1:
time: 188 us; the launch traced here: 186 us
  local copies, waits for them, and re-layouts  47.3 us (25%)
  waiting for transfers between devices  46 us (24%)
  starting transfers between devices  34.7 us (18%)
  other arithmetic  23.5 us (12%)
  blocking collectives  17.3 us (9%)
  matrix products  16.1 us (9%)
    all_to_all x3, waiting for transfers between devices, shuffled(): return lax.all_to_all(array, SPLIT, 0, 0, tiled=True)  46 us
    all_to_all x3, starting transfers between devices, shuffled(): return lax.all_to_all(array, SPLIT, 0, 0, tiled=True)  29.2 us
    all_to_all x1, blocking collectives, shuffled(): return lax.all_to_all(array, SPLIT, 0, 0, tiled=True)  17.3 us
    unnamed x72, local copies, waits for them, and re-layouts  14.7 us
    all_to_all x6, other arithmetic, shuffled(): return lax.all_to_all(array, SPLIT, 0, 0, tiled=True)  6.83 us
    dot_general x6, matrix products, dot32(): return jnp.einsum(spec, a, b, preferred_element_type=jnp.float32)  6.46 us
    all_to_all x4, local copies, waits for them, and re-layouts, shuffled(): return lax.all_to_all(array, SPLIT, 0, 0, tiled=True)  5.77 us
    ppermute x2, starting transfers between devices, swapped(): return lax.ppermute(array, 'co', [(0, 1), (1, 0)])  5.55 us
  transfers between devices with their start and end apart: 5, of which 3 were waited for; matrix products, arithmetic and copies ran while one was open for 11% of the time, Pallas kernels for 0%

profile of v1, /device:TPU:1, one launch (start us, length us, event | category | flops | bytes accessed | tf_op | source)
XLA Modules:
  0.0 186.4 jit_solution(3704581135759827269)
XLA Ops:
  0.6 1.2 convert_reduce_fusion
  1.9 1.6 fusion.15
  4.1 1.6 fusion.40
  9.9 1.7 reduce.4
  11.6 2.6 %reshape.202 = bf16[128,2,1152]{2,1,0:T(2,128)(2,1)} reshape(bf16[128,2304]{1,0:T(8,128)(2,1)} %reduce.4) | data formatting | bytes 1179648
  14.2 16.3 %all-to-all-start = ((bf16[128,2,1152]{2,1,0:T(2,128)(2,1)}), bf16[128,2,1152]{2,1,0:T(2,128)(2,1)S(1)}, u32[]{:S(2)}, u32[]{:S(2)}) async-start(bf16[128,2,1152]{2,1,0:T(2,128)(2,1)} %reshape.202), calls=%async_computation | async-start | bytes 1179648 | tf_op jit(solution)/shard_map/all_to_all | solution.py:48
  30.7 18.7 %all-to-all-done = bf16[128,2,1152]{2,1,0:T(2,128)(2,1)S(1)} async-done(((bf16[128,2,1152]{2,1,0:T(2,128)(2,1)}), bf16[128,2,1152]{2,1,0:T(2,128)(2,1)S(1)}, u32[]{:S(2)}, u32[]{:S(2)}) %all-to-all-start) | async-done | bytes 589856 | tf_op jit(solution)/shard_map/all_to_all | solution.py:48
  49.3 1.7 reshape.203
  51.1 1.3 copy.99
  52.5 1.4 reshape.185
  54.6 3.1 %collective-permute-start = (bf16[512,384]{0,1:T(8,128)(2,1)S(1)}, bf16[512,384]{0,1:T(8,128)(2,1)S(1)}, u32[]{:S(2)}, u32[]{:S(2)}) collective-permute-start(bf16[512,384]{0,1:T(8,128)(2,1)S(1)} %bitcast.122), channel_id=1, source_target_pairs={{0,32},{32,0},{1,33},{33,1},{2,34},{34,2},{3,35},{35,3},{4,36},{36... | collective-permute-start | bytes 1179656 | tf_op jit(solution)/shard_map/ppermute | solution.py:52
  57.7 1.9 %broadcast_select_fusion = (bf16[1,4,4,24,4,32]{5,3,2,0,1,4:T(8,128)(2,1)}, bf16[1,4,4,24,4,32]{5,3,2,0,1,4:T(8,128)(2,1)S(1)}) fusion(pred[]{:T(512)S(6)} %eq.2, bf16[2,4,4,24,4,32]{5,3,2,0,1,4:T(8,128)(2,1)} %bitcast.125), kind=kLoop, calls=%fused_computation.78 | loop fusion | flops 98304 | bytes 393217 | tf_op jit(solution)/shard_map/jit(_where)/select_n | solution.py:88
  60.6 1.9 %select_n.34 = bf16[384,128]{1,0:T(8,128)(2,1)} reshape(bf16[1,4,4,24,4,32]{5,4,3,2,1,0:T(4,128)(2,1)} %copy.73) | data formatting | bytes 196608 | tf_op jit(solution)/shard_map/jit(_where)/select_n | solution.py:87
  62.5 2.0 %copy.75 = bf16[1,4,4,24,4,32]{5,4,3,2,1,0:T(4,128)(2,1)} copy(bf16[1,4,4,24,4,32]{5,3,2,0,1,4:T(8,128)(2,1)} %get-tuple-element.16) | data formatting | bytes 196608 | tf_op jit(solution)/shard_map/jit(_where)/select_n | solution.py:88
  64.6 1.3 select_n.36
  65.8 1.2 fusion.109
  68.0 1.7 copy.76
  69.6 1.1 reshape.188
  70.8 1.8 copy.77
  72.6 1.4 all_to_all.31
  75.5 6.5 %all-to-all-start.1 = ((bf16[128,2,256]{2,1,0:T(2,128)(2,1)}), bf16[128,2,256]{2,1,0:T(2,128)(2,1)S(1)}, u32[]{:S(2)}, u32[]{:S(2)}) async-start(bf16[128,2,256]{2,1,0:T(2,128)(2,1)} %reshape.204), calls=%async_computation.1 | async-start | bytes 262144 | tf_op jit(solution)/shard_map/all_to_all | solution.py:48
  82.8 9.8 %all-to-all-done.1 = bf16[128,2,256]{2,1,0:T(2,128)(2,1)S(1)} async-done(((bf16[128,2,256]{2,1,0:T(2,128)(2,1)}), bf16[128,2,256]{2,1,0:T(2,128)(2,1)S(1)}, u32[]{:S(2)}, u32[]{:S(2)}) %all-to-all-start.1) | async-done | bytes 131104 | tf_op jit(solution)/shard_map/all_to_all | solution.py:48
  97.3 1.1 fusion.81
  98.4 2.0 %multiply_convert_fusion.3 = (bf16[32,16,128]{2,1,0:T(8,128)(2,1)}, f32[32,16,128]{2,1,0:T(8,128)S(1)}) fusion(f32[32,16,128]{2,1,0:T(8,128)S(1)} %fusion.81, bf16[128,128]{1,0:T(8,128)(2,1)} %param.18, bf16[32,16,128]{2,1,0:T(8,128)(2,1)} %param.14, f32[128]{0:T(128)} %param.21, f32[128]{0:T(128)} %param.20, f32[32,16]{1,0:T(8,128)} %add_rsqrt_fusion.1, ...), kind=kOutput, calls=%fused_computation.105 | convolution fusion | flops 17498112 | bytes 824320 | tf_op jit(solution)/shard_map/dot_general | solution.py:97
  100.5 1.4 fusion.108
  104.6 17.3 %all_to_all.42 = bf16[128,2,256]{2,1,0:T(2,128)(2,1)} all-to-all(bf16[128,2,256]{2,1,0:T(2,128)(2,1)S(1)} %reshape.206), channel_id=1, replica_groups=mesh['zl'=4,'co'=2,'y'=4,'x'=4,'zh'=2] {'zl','y','x','zh'}, dimensions={0} | all-to-all | bytes 262144 | tf_op jit(solution)/shard_map/all_to_all | solution.py:48
  122.0 1.4 reshape.207
  124.1 1.1 reshape.191
  125.3 1.8 copy.83
  127.1 1.4 reshape.192
  128.5 1.9 %convolution_convert_fusion = bf16[512,384]{0,1:T(8,128)(2,1)} fusion(bf16[128,512]{0,1:T(8,128)(2,1)S(1)} %reshape.192, bf16[384,128]{1,0:T(8,128)(2,1)} %copy-done.10), kind=kOutput, calls=%fused_computation.1 | convolution fusion | flops 50528256 | bytes 622592 | tf_op jit(solution)/shard_map/ij,ki->jk/dot_general | solution.py:56
  130.4 2.5 %collective-permute-start.1 = (bf16[512,384]{0,1:T(8,128)(2,1)}, bf16[512,384]{0,1:T(8,128)(2,1)}, u32[]{:S(2)}, u32[]{:S(2)}) collective-permute-start(bf16[512,384]{0,1:T(8,128)(2,1)} %convolution_convert_fusion), channel_id=1, source_target_pairs={{0,32},{32,0},{1,33},{33,1},{2,34},{34,2},{3,35},{35,3},{4,36},{36... | collective-permute-start | bytes 1179656 | tf_op jit(solution)/shard_map/ppermute | solution.py:52
  134.4 1.8 stack.10
  136.2 1.0 copy.85
  138.3 2.3 %reshape.193 = bf16[128,768]{1,0:T(8,128)(2,1)} reshape(bf16[4,4,2,4,24,32]{5,4,3,2,1,0:T(8,128)(2,1)} %maximum_bitcast_fusion) | data formatting | bytes 393216 | tf_op jit(solution)/shard_map/reshape | solution.py:125
  140.6 1.3 add_convert_fusion
  142.2 1.3 reshape.195
  143.5 1.1 maximum_bitcast_fusion.2
  144.6 1.7 reduce.7
  146.3 2.6 %reshape.208 = bf16[128,2,1152]{2,1,0:T(2,128)(2,1)} reshape(bf16[128,2304]{1,0:T(8,128)(2,1)} %reduce.7) | data formatting | bytes 1179648
  148.9 6.4 %all-to-all-start.3 = ((bf16[128,2,1152]{2,1,0:T(2,128)(2,1)}), bf16[128,2,1152]{2,1,0:T(2,128)(2,1)S(1)}, u32[]{:S(2)}, u32[]{:S(2)}) async-start(bf16[128,2,1152]{2,1,0:T(2,128)(2,1)} %reshape.208), calls=%async_computation.3 | async-start | bytes 1179648 | tf_op jit(solution)/shard_map/all_to_all | solution.py:48
  155.4 1.4 fusion.107
  157.8 17.5 %all-to-all-done.3 = bf16[128,2,1152]{2,1,0:T(2,128)(2,1)S(1)} async-done(((bf16[128,2,1152]{2,1,0:T(2,128)(2,1)}), bf16[128,2,1152]{2,1,0:T(2,128)(2,1)S(1)}, u32[]{:S(2)}, u32[]{:S(2)}) %all-to-all-start.3) | async-done | bytes 589856 | tf_op jit(solution)/shard_map/all_to_all | solution.py:48
  175.3 1.7 reshape.209
  177.1 3.0 %copy.89 = bf16[128,1,2304]{0,2,1:T(8,128)(2,1)S(1)} copy(bf16[128,1,2304]{2,1,0:T(2,128)(2,1)} %reshape.209) | data formatting | bytes 1179648 | tf_op jit(solution)/shard_map/all_to_all | solution.py:48
  181.1 1.1 fusion.105
  183.6 1.7 fusion.14
  185.3 1.2 fusion.38
  (124 shorter events, 24.0 us)
Async XLA Ops:
  0.6 3.5 %copy-start = (bf16[128,256]{1,0:T(8,128)(2,1)S(1)}, bf16[128,256]{1,0:T(8,128)(2,1)}, u32[]{:S(2)}) copy-start(bf16[128,256]{1,0:T(8,128)(2,1)} %param.17) | copy-start | bytes 196612
  1.9 1.6 copy-start.21
  3.5 0.6 copy-start.23
  5.7 1.2 copy-start.2
  5.7 1.7 copy-start.25
  5.8 1.7 copy-start.27
  5.8 1.7 copy-start.30
  7.1 1.0 copy-start.16
  7.5 0.6 copy-start.19
  11.6 19.0 %copy-start.3 = (bf16[32,16,128]{2,1,0:T(8,128)(2,1)S(1)}, bf16[32,16,128]{2,1,0:T(8,128)(2,1)}, u32[]{:S(2)}) copy-start(bf16[32,16,128]{2,1,0:T(8,128)(2,1)} %param.14) | copy-start | bytes 393220
  14.2 35.2 %all-to-all-start = ((bf16[128,2,1152]{2,1,0:T(2,128)(2,1)}), bf16[128,2,1152]{2,1,0:T(2,128)(2,1)S(1)}, u32[]{:S(2)}, u32[]{:S(2)}) async-start(bf16[128,2,1152]{2,1,0:T(2,128)(2,1)} %reshape.202), calls=%async_computation | async-start | bytes 1179648 | tf_op jit(solution)/shard_map/all_to_all | solution.py:48
  54.6 12.5 %collective-permute-start = (bf16[512,384]{0,1:T(8,128)(2,1)S(1)}, bf16[512,384]{0,1:T(8,128)(2,1)S(1)}, u32[]{:S(2)}, u32[]{:S(2)}) collective-permute-start(bf16[512,384]{0,1:T(8,128)(2,1)S(1)} %bitcast.122), channel_id=1, source_target_pairs={{0,32},{32,0},{1,33},{33,1},{2,34},{34,2},{3,35},{35,3},{4,36},{36... | collective-permute-start | bytes 1179656 | tf_op jit(solution)/shard_map/ppermute | solution.py:52
  65.8 2.1 %copy-start.10 = (bf16[384,128]{1,0:T(8,128)(2,1)}, bf16[384,128]{1,0:T(8,128)(2,1)S(1)}, u32[]{:S(2)}) copy-start(bf16[384,128]{1,0:T(8,128)(2,1)S(1)} %select_n.36) | copy-start | bytes 294916
  67.0 0.9 copy-start.6
  72.6 9.4 %copy-start.4 = (bf16[32,16,128]{2,1,0:T(8,128)(2,1)S(1)}, bf16[32,16,128]{2,1,0:T(8,128)(2,1)}, u32[]{:S(2)}) copy-start(bf16[32,16,128]{2,1,0:T(8,128)(2,1)} %param.14) | copy-start | bytes 393220
  75.5 17.2 %all-to-all-start.1 = ((bf16[128,2,256]{2,1,0:T(2,128)(2,1)}), bf16[128,2,256]{2,1,0:T(2,128)(2,1)S(1)}, u32[]{:S(2)}, u32[]{:S(2)}) async-start(bf16[128,2,256]{2,1,0:T(2,128)(2,1)} %reshape.204), calls=%async_computation.1 | async-start | bytes 262144 | tf_op jit(solution)/shard_map/all_to_all | solution.py:48
  95.6 1.1 copy-start.12
  96.7 0.6 copy-start.14
  98.4 2.1 %copy-start.9 = (f32[32,16,128]{2,1,0:T(8,128)}, f32[32,16,128]{2,1,0:T(8,128)S(1)}, u32[]{:S(2)}) copy-start(f32[32,16,128]{2,1,0:T(8,128)S(1)} %fusion.81) | copy-start | bytes 786436
  98.4 2.1 %copy-start.13 = (f32[32,16]{1,0:T(8,128)S(1)}, f32[32,16]{1,0:T(8,128)}, u32[]{:S(2)}) copy-start(f32[32,16]{1,0:T(8,128)} %copy-done.12) | copy-start | bytes 6148
  98.4 2.1 %copy-start.15 = (f32[32,16]{1,0:T(8,128)S(1)}, f32[32,16]{1,0:T(8,128)}, u32[]{:S(2)}) copy-start(f32[32,16]{1,0:T(8,128)} %copy-done.14) | copy-start | bytes 6148
  100.5 4.2 %copy-start.8 = (f32[32,16,128]{2,1,0:T(8,128)}, f32[32,16,128]{2,1,0:T(8,128)S(1)}, u32[]{:S(2)}) copy-start(f32[32,16,128]{2,1,0:T(8,128)S(1)} %get-tuple-element.21) | copy-start | bytes 786436
  127.1 6.1 %copy-start.7 = (bf16[512,384]{0,1:T(8,128)(2,1)S(1)}, bf16[512,384]{0,1:T(8,128)(2,1)}, u32[]{:S(2)}) copy-start(bf16[512,384]{0,1:T(8,128)(2,1)} %copy-done.6) | copy-start | bytes 1179652
  130.4 10.2 %collective-permute-start.1 = (bf16[512,384]{0,1:T(8,128)(2,1)}, bf16[512,384]{0,1:T(8,128)(2,1)}, u32[]{:S(2)}, u32[]{:S(2)}) collective-permute-start(bf16[512,384]{0,1:T(8,128)(2,1)} %convolution_convert_fusion), channel_id=1, source_target_pairs={{0,32},{32,0},{1,33},{33,1},{2,34},{34,2},{3,35},{35,3},{4,36},{36... | collective-permute-start | bytes 1179656 | tf_op jit(solution)/shard_map/ppermute | solution.py:52
  146.3 9.0 %copy-start.5 = (bf16[32,16,128]{2,1,0:T(8,128)(2,1)S(1)}, bf16[32,16,128]{2,1,0:T(8,128)(2,1)}, u32[]{:S(2)}) copy-start(bf16[32,16,128]{2,1,0:T(8,128)(2,1)} %param.14) | copy-start | bytes 393220
  146.3 9.0 %copy-start.11 = (bf16[32,16,128]{2,1,0:T(8,128)(2,1)S(1)}, bf16[32,16,128]{2,1,0:T(8,128)(2,1)}, u32[]{:S(2)}) copy-start(bf16[32,16,128]{2,1,0:T(8,128)(2,1)} %param.15) | copy-start | bytes 393220
  146.3 9.1 %copy-start.18 = (f32[32,16]{1,0:T(8,128)S(1)}, f32[32,16]{1,0:T(8,128)}, u32[]{:S(2)}) copy-start(f32[32,16]{1,0:T(8,128)} %add_rsqrt_fusion.1) | copy-start | bytes 6148
  146.3 9.1 %copy-start.28 = (f32[128]{0:T(128)S(1)}, f32[128]{0:T(128)}, u32[]{:S(2)}) copy-start(f32[128]{0:T(128)} %param.20) | copy-start | bytes 1540
  148.9 26.4 %all-to-all-start.3 = ((bf16[128,2,1152]{2,1,0:T(2,128)(2,1)}), bf16[128,2,1152]{2,1,0:T(2,128)(2,1)S(1)}, u32[]{:S(2)}, u32[]{:S(2)}) async-start(bf16[128,2,1152]{2,1,0:T(2,128)(2,1)} %reshape.208), calls=%async_computation.3 | async-start | bytes 1179648 | tf_op jit(solution)/shard_map/all_to_all | solution.py:48
  180.1 1.0 copy-start.1
  180.1 1.0 copy-start.22
  180.1 1.0 copy-start.24
  180.1 1.0 copy-start.29
  182.2 0.7 copy-start.17
  182.2 0.7 copy-start.20
  182.2 0.9 copy-start.26

commit v2 on v1

v2 whole, which is shorter than its diff:
```python
import functools

import jax
import jax.numpy as jnp
from jax import lax
from jax.experimental import pallas as pl
from jax.experimental.pallas import tpu as pltpu
from jax.sharding import Mesh
from jax.sharding import PartitionSpec as P

IA = ("zl", "co")
JA = ("y", "x", "zh")
SPLIT = ("zl", "y", "x", "zh")

epsilon = 1e-05
F32 = jnp.float32
BF16 = jnp.bfloat16


def stats(values):
    centre = jnp.mean(values, axis=-1, keepdims=True)
    shifted = values - centre
    inverse = lax.rsqrt(jnp.mean(shifted * shifted, axis=-1, keepdims=True) + epsilon)
    return shifted * inverse, inverse


def norm_back(scaled, inverse, grad_out, gain):
    grad_hat = grad_out * gain
    first_mean = jnp.mean(grad_hat, axis=-1, keepdims=True)
    second_mean = jnp.mean(grad_hat * scaled, axis=-1, keepdims=True)
    return inverse * (grad_hat - first_mean - scaled * second_mean)


def dot(a, b, dims=((1,), (0,))):
    return lax.dot_general(a, b, (dims, ((), ())), preferred_element_type=F32)


def edges(rows, weights, gain, bias):
    scaled, inverse = stats(rows.astype(F32))
    hidden = dot((scaled * gain + bias).astype(BF16), weights)
    return hidden[:, :128], jax.nn.sigmoid(hidden[:, 128:]), scaled, inverse


def lane_group(shape):
    return lax.broadcasted_iota(jnp.int32, shape, 1) // 32


def moved(block, source, target):
    shift = ((target - source) * 32) % 128
    return block if shift == 0 else pltpu.roll(block, shift, 1)


def project_kernel(slab, column, w_left, w_right, gain, bias, out, left_rows, chunks):
    g, b = gain[...], bias[...]
    for step in range(8):
        rows = pl.ds(step * 96, 96)
        linear, sigma, _, _ = edges(slab[rows, :], w_left[...], g, b)
        left_rows[rows, :] = sigma * linear
    for r in range(24):
        left_part = left_rows[pl.ds(r, 32, stride=24), :]
        if r < 16:
            linear, sigma, _, _ = edges(column[pl.ds(r * 96, 96), :], w_right[...], g, b)
            right_part = sigma * linear
        else:
            right_part = jnp.zeros((96, 128), F32)
        block = jnp.concatenate([right_part, left_part], axis=0)
        chunks[pl.ds(r, 128, stride=24), :] = block.T
    out[...] = chunks[...].astype(BF16)


def right_of(chunk):
    rows = chunk.astype(F32).reshape(32, 24, 128)[:, :16, :].reshape(512, 128)
    return rows.astype(BF16)


def padded(rows):
    return jnp.concatenate([rows, jnp.zeros((32, 128), BF16)], axis=0)


def left_block(left, zl, core):
    start = pl.multiple_of((2 * zl + core) * 96, 32)
    return padded(left[pl.ds(start, 96), :])


def first_product_kernel(core, got, left, right, partial):
    group = lane_group((768, 128))
    merged = None
    for zl in range(4):
        chunk = got[pl.ds(zl * 768, 768), :]
        piece = moved(chunk.astype(F32), 3, zl)
        merged = piece if merged is None else jnp.where(group == zl, piece, merged)
        right[pl.ds(zl * 512, 512), :] = right_of(chunk)
    left[...] = merged.astype(BF16)
    total = None
    for zl in range(4):
        term = dot(right[pl.ds(zl * 512, 512), :], left_block(left, zl, core[0]))
        total = term if total is None else total + term
    partial[...] = total


def second_product_kernel(core, come, left, partial, right, out, total):
    acc = partial[...]
    for zl in range(4):
        chunk = right_of(come[pl.ds(zl * 768, 768), :])
        right[pl.ds(zl * 512, 512), :] = chunk
        acc = acc + dot(chunk, left_block(left, zl, 1 - core[0]))
    total[...] = acc
    group = lane_group((128, 128))
    parts = [total[pl.ds(jl, 128, stride=4), :] for jl in range(4)]
    for zl in range(4):
        merged = moved(parts[0], zl, 0)
        for jl in range(1, 4):
            merged = jnp.where(group == jl, moved(parts[jl], zl, jl), merged)
        out[pl.ds(zl * 128, 128), :] = merged.astype(BF16)


def gate_kernel(tile, cotangent, gate_w, out_w, gain, bias, u_gain, gate_out, eg_out, rows, cots):
    scaled, _ = stats(tile[...].astype(F32))
    gate = jax.nn.sigmoid(
        dot((scaled * gain[...] + bias[...]).astype(BF16), gate_w[...])
    )
    gate_out[...] = gate
    grad_outer = (cotangent[...].astype(F32) * gate).astype(BF16)
    rows[...] = dot(grad_outer, out_w[...], ((1,), (1,))) * u_gain[...]
    for jh in range(4):
        block = jnp.concatenate(
            [rows[pl.ds(4 * jh + jl, 32, stride=16), :] for jl in range(4)], axis=0
        )
        eg_out[pl.ds(jh * 128, 128), :] = block.T


def tri_back_kernel(tri, eg, out, tri_rows, d_rows):
    tri_rows[...] = tri[...].astype(F32)
    for jh in range(4):
        value = tri_rows[pl.ds(jh, 128, stride=4), :]
        centre = jnp.mean(value, axis=0, keepdims=True)
        shifted = value - centre
        inverse = lax.rsqrt(jnp.mean(shifted * shifted, axis=0, keepdims=True) + epsilon)
        scaled = shifted * inverse
        grad_hat = eg[pl.ds(jh * 128, 128), :]
        first_mean = jnp.mean(grad_hat, axis=0, keepdims=True)
        second_mean = jnp.mean(grad_hat * scaled, axis=0, keepdims=True)
        d_rows[pl.ds(jh, 128, stride=4), :] = inverse * (
            grad_hat - first_mean - scaled * second_mean
        )
    out[...] = d_rows[...].astype(BF16)


def tile_kernel(
    tri, tile, cotangent, gate_in, gate_w, out_w, gain, bias, u_gain, u_bias,
    update, grad_tile, tri_rows, run_rows,
):
    tri_rows[...] = tri[...].astype(F32)
    for jh in range(4):
        block = tri_rows[pl.ds(jh, 128, stride=4), :].T
        for jl in range(4):
            run_rows[pl.ds(4 * jh + jl, 32, stride=16), :] = block[jl * 32 : jl * 32 + 32, :]
    tri_scaled, _ = stats(run_rows[...])
    outer = dot((tri_scaled * u_gain[...] + u_bias[...]).astype(BF16), out_w[...])
    gate = gate_in[...]
    update[...] = (gate * outer).astype(BF16)
    grad_gate = (cotangent[...].astype(F32) * outer * gate * (1.0 - gate)).astype(BF16)
    grad_norm = dot(grad_gate, gate_w[...], ((1,), (1,)))
    scaled, inverse = stats(tile[...].astype(F32))
    grad_tile[...] = norm_back(scaled, inverse, grad_norm, gain[...]).astype(BF16)


def third_product_kernel(core, d_got, left, d_tri, d_right, d_rows):
    group = lane_group((128, 128))
    parts = [d_got[pl.ds(zl * 128, 128), :].astype(F32) for zl in range(4)]
    for jl in range(4):
        merged = moved(parts[0], jl, 0)
        for zl in range(1, 4):
            merged = jnp.where(group == zl, moved(parts[zl], jl, zl), merged)
        d_rows[pl.ds(jl, 128, stride=4), :] = merged
    d_now = d_rows[...].astype(BF16)
    d_tri[...] = d_now
    for zl in range(4):
        block = dot(d_now, left_block(left, zl, 1 - core[0]), ((1,), (1,)))
        d_right[pl.ds(zl * 512, 512), :] = block.astype(BF16)


def fourth_product_kernel(core, d_tri, right_own, right_other, d_left):
    d_t = d_tri[...].astype(F32).T.astype(BF16)
    for zl in range(4):
        for right, which in ((right_own, core[0]), (right_other, 1 - core[0])):
            block = dot(d_t, right[pl.ds(zl * 512, 512), :]).T
            start = pl.multiple_of((2 * zl + which) * 96, 32)
            d_left[pl.ds(start, 96), :] = block[:96, :]


def fifth_product_kernel(core, d_tri, left, come, d_left, out):
    d_now = d_tri[...]
    is_left = lane_group((768, 128)) == 3
    for zl in range(4):
        block = dot(d_now, left_block(left, zl, core[0]), ((1,), (1,)))
        block = block + come[pl.ds(zl * 512, 512), :].astype(F32)
        block = jnp.concatenate(
            [block.reshape(32, 16, 128), jnp.zeros((32, 8, 128), F32)], axis=1
        ).reshape(768, 128)
        merged = jnp.where(is_left, moved(d_left[...], zl, 3), block)
        out[pl.ds(zl * 768, 768), :] = merged.astype(BF16)


def edges_back(grad_edge, rows, weights, gain, bias):
    linear, sigma, scaled, inverse = edges(rows, weights, gain, bias)
    joined = jnp.concatenate(
        [grad_edge * sigma, grad_edge * linear * sigma * (1.0 - sigma)], axis=1
    )
    grad_norm = dot(joined.astype(BF16), weights, ((1,), (1,)))
    return norm_back(scaled, inverse, grad_norm, gain).astype(BF16)


def project_back_kernel(
    back, slab, column, w_left, w_right, gain, bias, grad_slab, grad_column, chunks, left_rows
):
    g, b = gain[...], bias[...]
    chunks[...] = back[...].astype(F32)
    for r in range(24):
        block = chunks[pl.ds(r, 128, stride=24), :].T
        left_rows[pl.ds(r, 32, stride=24), :] = block[96:, :]
        if r < 16:
            rows = pl.ds(r * 96, 96)
            grad_column[rows, :] = edges_back(block[:96, :], column[rows, :], w_right[...], g, b)
    for step in range(8):
        rows = pl.ds(step * 96, 96)
        grad_slab[rows, :] = edges_back(left_rows[rows, :], slab[rows, :], w_left[...], g, b)


VMEM = pl.BlockSpec(memory_space=pltpu.VMEM)
SMEM = pl.BlockSpec(memory_space=pltpu.SMEM)


def run(kernel, name, outs, scratch, *args, flops=100_000_000, moved_bytes=2_000_000):
    return pl.pallas_call(
        kernel,
        name=name,
        out_shape=[jax.ShapeDtypeStruct(s, t) for s, t in outs],
        in_specs=[SMEM if a.dtype == jnp.int32 else VMEM for a in args],
        out_specs=[VMEM] * len(outs),
        scratch_shapes=[pltpu.VMEM((n, 128), F32) for n in scratch],
        cost_estimate=pl.CostEstimate(
            flops=flops, bytes_accessed=moved_bytes, transcendentals=0
        ),
    )(*args)


def shuffled(array):
    rows = array.shape[0] // 128
    return lax.all_to_all(array.reshape(128, rows, 128), SPLIT, 0, 0, tiled=True).reshape(
        array.shape
    )


def swapped(array):
    return lax.ppermute(array, "co", [(0, 1), (1, 0)])


def shards(
    slab_rows,
    column_rows,
    pair_tile,
    cotangent,
    weights_left,
    weights_right,
    gate_weight,
    out_weight,
    input_gain,
    input_bias,
    update_gain,
    update_bias,
):
    core = lax.axis_index("co").astype(jnp.int32).reshape(1)
    slab = slab_rows.reshape(768, 128)
    column = column_rows.reshape(1536, 128)
    tile = pair_tile.reshape(512, 128)
    cots = cotangent.reshape(512, 128)
    gain, bias, u_gain, u_bias = (
        v.reshape(1, 128) for v in (input_gain, input_bias, update_gain, update_bias)
    )
    (sent,) = run(
        project_kernel, "project", [((3072, 128), BF16)], [768, 3072],
        slab, column, weights_left, weights_right, gain, bias,
    )
    got = shuffled(sent)
    gate, eg = run(
        gate_kernel, "gate", [((512, 128), F32)] * 2, [512, 512],
        tile, cots, gate_weight, out_weight, gain, bias, u_gain,
    )
    come = swapped(got)
    left, right_own, partial = run(
        first_product_kernel, "product_one",
        [((768, 128), BF16), ((2048, 128), BF16), ((512, 128), F32)], [], core, got,
    )
    right_other, tri_sent = run(
        second_product_kernel, "product_two",
        [((2048, 128), BF16), ((512, 128), BF16)], [512], core, come, left, partial,
    )
    tri = shuffled(tri_sent)
    (d_sent,) = run(tri_back_kernel, "tri_back", [((512, 128), BF16)], [512, 512], tri, eg)
    d_got = shuffled(d_sent)
    update, grad_tile = run(
        tile_kernel, "tile", [((512, 128), BF16)] * 2, [512, 512],
        tri, tile, cots, gate, gate_weight, out_weight, gain, bias, u_gain, u_bias,
    )
    d_tri, d_right_other = run(
        third_product_kernel, "product_three",
        [((512, 128), BF16), ((2048, 128), BF16)], [512], core, d_got, left,
    )
    d_right_come = swapped(d_right_other)
    (d_left,) = run(
        fourth_product_kernel, "product_four", [((768, 128), F32)], [],
        core, d_tri, right_own, right_other,
    )
    (back_sent,) = run(
        fifth_product_kernel, "product_five", [((3072, 128), BF16)], [],
        core, d_tri, left, d_right_come, d_left,
    )
    back = shuffled(back_sent)
    grad_slab, grad_column = run(
        project_back_kernel, "project_back",
        [((768, 128), BF16), ((1536, 128), BF16)], [3072, 768],
        back, slab, column, weights_left, weights_right, gain, bias,
    )
    return (
        update.reshape(pair_tile.shape),
        grad_slab.reshape(slab_rows.shape),
        grad_column.reshape(column_rows.shape),
        grad_tile.reshape(pair_tile.shape),
    )


def solution(mesh):
    finer = Mesh(mesh.devices.reshape(4, 2, 4, 4, 2), ("zl", "co", "y", "x", "zh"))
    row_spec = P(IA, JA, None)
    column_spec = P(JA, IA, None)
    in_specs = (row_spec, column_spec, row_spec, row_spec) + (P(),) * 8
    return jax.shard_map(
        shards,
        mesh=finer,
        in_specs=in_specs,
        out_specs=(row_spec, row_spec, column_spec, row_spec),
        check_vma=False,
    )
```

time: 188 us -> 139 us (0.74)
  local copies, waits for them, and re-layouts: 47.3 us -> 3.27 us
  blocking collectives: 17.3 us -> 57 us
  Pallas kernels: 0 us -> 28.3 us
  other arithmetic: 23.5 us -> 0 us
  waiting for transfers between devices: 46 us -> 29.5 us
  matrix products: 16.1 us -> 0 us
  starting transfers between devices: 34.7 us -> 19.5 us
    all_to_all x1 -> x2, blocking collectives: 17.3 us -> 57 us  [shuffled(): lax.all_to_all(array.reshape(128, rows, 128), SPLIT, 0, 0, tiled=True)]
    pallas_call x0 -> x10, Pallas kernels: none -> 28.3 us  [run(): pl.pallas_call(kernel, name=name, out_shape=[jax.ShapeDtypeStruct(s, t) f...]
    all_to_all x3 -> x2, waiting for transfers between devices: 46 us -> 29.5 us  [shuffled(): lax.all_to_all(array.reshape(128, rows, 128), SPLIT, 0, 0, tiled=True)]
    all_to_all x3 -> x2, starting transfers between devices: 29.2 us -> 12.9 us  [shuffled(): lax.all_to_all(array.reshape(128, rows, 128), SPLIT, 0, 0, tiled=True)]
    dot_general x14 -> x0, matrix products: 16.1 us -> none  [the longest x6 6.46 us: dot32(): return jnp.einsum(spec, a, b, preferred_element_type=jnp.float32)]
    reshape x11 -> x0, local copies, waits for them, and re-layouts: 11.6 us -> none  [the longest x1 2.35 us: shards(): jnp.transpose(d_left.reshape(2, 4, 4, 24, 4, 32), (4, 1, 0, 2, 3, 5))]
    unnamed x72 -> x10, local copies, waits for them, and re-layouts: 14.7 us -> 3.27 us
    all_to_all x6 -> x0, other arithmetic: 6.83 us -> none  [shuffled(): return lax.all_to_all(array, SPLIT, 0, 0, tiled=True)]
  transfers between devices with their start and end apart: 5 -> 4, of which waited for: 3 -> 2; matrix products, arithmetic and copies ran while one was open for 11% -> 0% of each run, Pallas kernels for 0% -> 7%
where the time goes in v2:
time: 139 us; the launch traced here: 138 us
  blocking collectives  57 us (41%)
  waiting for transfers between devices  29.5 us (21%)
  Pallas kernels  28.3 us (20%)
  starting transfers between devices  19.5 us (14%)
  local copies, waits for them, and re-layouts  3.27 us (2%)
    all_to_all x2, blocking collectives, shuffled(): lax.all_to_all(array.reshape(128, rows, 128), SPLIT, 0, 0, tiled=True)  57 us
    all_to_all x2, waiting for transfers between devices, shuffled(): lax.all_to_all(array.reshape(128, rows, 128), SPLIT, 0, 0, tiled=True)  29.5 us
    pallas_call x10, Pallas kernels, run(): pl.pallas_call(kernel, name=name, out_shape=[jax.ShapeDtypeStruct(s, t) f...  28.3 us
    all_to_all x2, starting transfers between devices, shuffled(): lax.all_to_all(array.reshape(128, rows, 128), SPLIT, 0, 0, tiled=True)  12.9 us
    ppermute x2, starting transfers between devices, swapped(): return lax.ppermute(array, 'co', [(0, 1), (1, 0)])  6.6 us
    unnamed x10, local copies, waits for them, and re-layouts  3.27 us
  transfers between devices with their start and end apart: 4, of which 2 were waited for; matrix products, arithmetic and copies ran while one was open for 0% of the time, Pallas kernels for 7%

profile of v2, /device:TPU:1, one launch (start us, length us, event | category | flops | bytes accessed | tf_op | source)
XLA Modules:
  0.0 138.2 jit_solution(2459595425637267170)
XLA Ops:
  0.6 4.5 %project.1 = bf16[3072,128]{1,0:T(8,128)(2,1)} custom-call(bf16[768,128]{1,0:T(8,128)(2,1)} %bitcast.30, bf16[1536,128]{1,0:T(8,128)(2,1)} %bitcast.26, bf16[128,256]{1,0:T(8,128)(2,1)} %w_left.3, bf16[128,256]{1,0:T(8,128)(2,1)} %w_right.3, f32[1,128]{1,0:T(1,128)} %bitcast.39, f32[1,128]{1,0:T(1,128)} %bitcast.43), custom_call_target="tpu_custom_call" | custom-call | flops 100000000 | bytes 2000000 | tf_op jit(solution)/shard_map/project/pallas_call | solution.py:235
  5.1 39.3 %all_to_all.20 = bf16[128,24,128]{2,1,0:T(8,128)(2,1)S(1)} all-to-all(bf16[128,24,128]{2,1,0:T(8,128)(2,1)} %bitcast.25), channel_id=1, replica_groups=mesh['zl'=4,'co'=2,'y'=4,'x'=4,'zh'=2] {'zl','y','x','zh'}, dimensions={0} | all-to-all | bytes 1572864 | tf_op jit(solution)/shard_map/all_to_all | solution.py:250
  44.4 0.0 copy-start
  44.4 3.1 %collective-permute-start = (bf16[3072,128]{1,0:T(8,128)(2,1)S(1)}, bf16[3072,128]{1,0:T(8,128)(2,1)S(1)}, u32[]{:S(2)}, u32[]{:S(2)}) collective-permute-start(bf16[3072,128]{1,0:T(8,128)(2,1)S(1)} %bitcast.21), channel_id=1, source_target_pairs={{0,32},{32,0},{1,33},{33,1},{2,34},{34,2},{3,35},{35,3},{4,36},{36... | collective-permute-start | bytes 2359304 | tf_op jit(solution)/shard_map/ppermute | solution.py:256
  47.5 0.0 copy-done
  47.5 2.4 %product_one.1 = (bf16[768,128]{1,0:T(8,128)(2,1)}, bf16[2048,128]{1,0:T(8,128)(2,1)}, f32[512,128]{1,0:T(8,128)}) custom-call(s32[1]{0:T(128)} %bitcast.core, bf16[3072,128]{1,0:T(8,128)(2,1)} %bitcast.22), custom_call_target="tpu_custom_call" | custom-call | flops 100000000 | bytes 2000000 | tf_op jit(solution)/shard_map/product_one/pallas_call | solution.py:235
  49.8 0.0 collective-permute-done.come
  49.8 0.0 copy-start.3
  49.8 0.9 copy-done.3
  50.7 2.4 %product_two.1 = (bf16[2048,128]{1,0:T(8,128)(2,1)}, bf16[512,128]{1,0:T(8,128)(2,1)}) custom-call(s32[1]{0:T(128)} %bitcast.core, bf16[3072,128]{1,0:T(8,128)(2,1)} %copy-done.3, bf16[768,128]{1,0:T(8,128)(2,1)} %get-tuple-element.17.left, f32[512,128]{1,0:T(8,128)} %get-tuple-element.18.partial), custom_call_target="tpu_custom_call" | custom-call | flops 100000000 | bytes 2000000 | tf_op jit(solution)/shard_map/product_two/pallas_call | solution.py:235
  53.1 6.5 %all-to-all-start.1 = ((bf16[128,4,128]{2,1,0:T(4,128)(2,1)}), bf16[128,4,128]{2,1,0:T(4,128)(2,1)S(1)}, u32[]{:S(2)}, u32[]{:S(2)}) async-start(bf16[128,4,128]{2,1,0:T(4,128)(2,1)} %bitcast.33), calls=%async_computation.1 | async-start | bytes 262144 | tf_op jit(solution)/shard_map/all_to_all | solution.py:250
  59.7 2.4 %gate.1 = (f32[512,128]{1,0:T(8,128)}, f32[512,128]{1,0:T(8,128)}) custom-call(bf16[512,128]{1,0:T(8,128)(2,1)} %bitcast.35, bf16[512,128]{1,0:T(8,128)(2,1)} %bitcast.37, bf16[128,128]{1,0:T(8,128)(2,1)} %gate_w.3, bf16[128,128]{1,0:T(8,128)(2,1)} %out_w.3, f32[1,128]{1,0:T(1,128)} %bitcast.40, f32[1,128]{1,0:T(1,128)} %bitcast.44, f32[1,128]{1,0:T(1,128)} %bitcast.47), custom_call_target="tpu_custom_call" | custom-call | flops 100000000 | bytes 2000000 | tf_op jit(solution)/shard_map/gate/pallas_call | solution.py:235
  62.0 7.9 %all-to-all-done.1 = bf16[128,4,128]{2,1,0:T(4,128)(2,1)S(1)} async-done(((bf16[128,4,128]{2,1,0:T(4,128)(2,1)}), bf16[128,4,128]{2,1,0:T(4,128)(2,1)S(1)}, u32[]{:S(2)}, u32[]{:S(2)}) %all-to-all-start.1) | async-done | bytes 131104 | tf_op jit(solution)/shard_map/all_to_all | solution.py:250
  69.9 0.0 copy-start.2
  69.9 0.6 copy-done.2
  70.6 1.9 %tri_back.1 = bf16[512,128]{1,0:T(8,128)(2,1)} custom-call(bf16[512,128]{1,0:T(8,128)(2,1)} %bitcast.28, f32[512,128]{1,0:T(8,128)} %get-tuple-element.22.eg), custom_call_target="tpu_custom_call" | custom-call | flops 100000000 | bytes 2000000 | tf_op jit(solution)/shard_map/tri_back/pallas_call | solution.py:235
  72.4 17.7 %all_to_all.21 = bf16[128,4,128]{2,1,0:T(4,128)(2,1)} all-to-all(bf16[128,4,128]{2,1,0:T(4,128)(2,1)} %bitcast.32), channel_id=1, replica_groups=mesh['zl'=4,'co'=2,'y'=4,'x'=4,'zh'=2] {'zl','y','x','zh'}, dimensions={0} | all-to-all | bytes 262144 | tf_op jit(solution)/shard_map/all_to_all | solution.py:250
  90.2 2.2 %product_three.1 = (bf16[512,128]{1,0:T(8,128)(2,1)}, bf16[2048,128]{1,0:T(8,128)(2,1)}) custom-call(s32[1]{0:T(128)} %bitcast.core, bf16[512,128]{1,0:T(8,128)(2,1)} %bitcast.34, bf16[768,128]{1,0:T(8,128)(2,1)} %get-tuple-element.17.left), custom_call_target="tpu_custom_call" | custom-call | flops 100000000 | bytes 2000000 | tf_op jit(solution)/shard_map/product_three/pallas_call | solution.py:235
  92.3 3.5 %collective-permute-start.1 = (bf16[2048,128]{1,0:T(8,128)(2,1)}, bf16[2048,128]{1,0:T(8,128)(2,1)S(1)}, u32[]{:S(2)}, u32[]{:S(2)}) collective-permute-start(bf16[2048,128]{1,0:T(8,128)(2,1)} %get-tuple-element.24), channel_id=1, source_target_pairs={{0,32},{32,0},{1,33},{33,1},{2,34},{34,2},{3,35},{35,3},{4,36},{36... | collective-permute-start | bytes 1572872 | tf_op jit(solution)/shard_map/ppermute | solution.py:256
  95.9 2.5 %product_four.1.d_left = f32[768,128]{1,0:T(8,128)} custom-call(s32[1]{0:T(128)} %bitcast.core, bf16[512,128]{1,0:T(8,128)(2,1)} %get-tuple-element.23.d_tri, bf16[2048,128]{1,0:T(8,128)(2,1)} %get-tuple-element.25.right_own, bf16[2048,128]{1,0:T(8,128)(2,1)} %get-tuple-element.26.right_other), custom_call_target="tpu_custom_call" | custom-call | flops 100000000 | bytes 2000000 | tf_op jit(solution)/shard_map/product_four/pallas_call | solution.py:235
  98.4 0.0 collective-permute-done.1.come
  98.4 0.0 copy-start.4
  98.4 0.8 copy-done.4
  99.2 2.6 %product_five.1 = bf16[3072,128]{1,0:T(8,128)(2,1)} custom-call(s32[1]{0:T(128)} %bitcast.core, bf16[512,128]{1,0:T(8,128)(2,1)} %get-tuple-element.23.d_tri, bf16[768,128]{1,0:T(8,128)(2,1)} %get-tuple-element.17.left, bf16[2048,128]{1,0:T(8,128)(2,1)} %copy-done.4, f32[768,128]{1,0:T(8,128)} %product_four.1.d_left), custom_call_target="tpu_custom_call" | custom-call | flops 100000000 | bytes 2000000 | tf_op jit(solution)/shard_map/product_five/pallas_call | solution.py:235
  101.8 6.4 %all-to-all-start.3 = ((bf16[128,24,128]{2,1,0:T(8,128)(2,1)}), bf16[128,24,128]{2,1,0:T(8,128)(2,1)S(1)}, u32[]{:S(2)}, u32[]{:S(2)}) async-start(bf16[128,24,128]{2,1,0:T(8,128)(2,1)} %bitcast.24), calls=%async_computation.3 | async-start | bytes 1572864 | tf_op jit(solution)/shard_map/all_to_all | solution.py:250
  108.2 2.6 %tile.1 = (bf16[512,128]{1,0:T(8,128)(2,1)}, bf16[512,128]{1,0:T(8,128)(2,1)}) custom-call(bf16[512,128]{1,0:T(8,128)(2,1)} %bitcast.29, bf16[512,128]{1,0:T(8,128)(2,1)} %bitcast.36, bf16[512,128]{1,0:T(8,128)(2,1)} %bitcast.38, f32[512,128]{1,0:T(8,128)} %get-tuple-element.20.gate_in, bf16[128,128]{1,0:T(8,128)(2,1)} %gate_w.3, bf16[128,128]{1,0:T(8,128)(2,1)} %out_w.3, ...), custom_call_target="tpu_custom_call" | custom-call | flops 100000000 | bytes 2000000 | tf_op jit(solution)/shard_map/tile/pallas_call | solution.py:235
  110.8 21.6 %all-to-all-done.3 = bf16[128,24,128]{2,1,0:T(8,128)(2,1)S(1)} async-done(((bf16[128,24,128]{2,1,0:T(8,128)(2,1)}), bf16[128,24,128]{2,1,0:T(8,128)(2,1)S(1)}, u32[]{:S(2)}, u32[]{:S(2)}) %all-to-all-start.3) | async-done | bytes 786464 | tf_op jit(solution)/shard_map/all_to_all | solution.py:250
  132.4 0.0 copy-start.1
  132.4 0.9 copy-done.1
  133.3 4.9 %project_back.1 = (bf16[768,128]{1,0:T(8,128)(2,1)}, bf16[1536,128]{1,0:T(8,128)(2,1)}) custom-call(bf16[3072,128]{1,0:T(8,128)(2,1)} %bitcast.23, bf16[768,128]{1,0:T(8,128)(2,1)} %bitcast.31, bf16[1536,128]{1,0:T(8,128)(2,1)} %bitcast.27, bf16[128,256]{1,0:T(8,128)(2,1)} %w_left.3, bf16[128,256]{1,0:T(8,128)(2,1)} %w_right.3, f32[1,128]{1,0:T(1,128)} %bitcast.42, ...), custom_call_target="tpu_custom_call" | custom-call | flops 100000000 | bytes 2000000 | tf_op jit(solution)/shard_map/project_back/pallas_call | solution.py:235
Async XLA Ops:
  44.4 3.1 %copy-start = (bf16[128,24,128]{2,1,0:T(8,128)(2,1)}, bf16[128,24,128]{2,1,0:T(8,128)(2,1)S(1)}, u32[]{:S(2)}) copy-start(bf16[128,24,128]{2,1,0:T(8,128)(2,1)S(1)} %all_to_all.20) | copy-start | bytes 2359300
  44.4 5.5 %collective-permute-start = (bf16[3072,128]{1,0:T(8,128)(2,1)S(1)}, bf16[3072,128]{1,0:T(8,128)(2,1)S(1)}, u32[]{:S(2)}, u32[]{:S(2)}) collective-permute-start(bf16[3072,128]{1,0:T(8,128)(2,1)S(1)} %bitcast.21), channel_id=1, source_target_pairs={{0,32},{32,0},{1,33},{33,1},{2,34},{34,2},{3,35},{35,3},{4,36},{36... | collective-permute-start | bytes 2359304 | tf_op jit(solution)/shard_map/ppermute | solution.py:256
  49.8 0.9 copy-start.3
  53.1 16.8 %all-to-all-start.1 = ((bf16[128,4,128]{2,1,0:T(4,128)(2,1)}), bf16[128,4,128]{2,1,0:T(4,128)(2,1)S(1)}, u32[]{:S(2)}, u32[]{:S(2)}) async-start(bf16[128,4,128]{2,1,0:T(4,128)(2,1)} %bitcast.33), calls=%async_computation.1 | async-start | bytes 262144 | tf_op jit(solution)/shard_map/all_to_all | solution.py:250
  69.9 0.7 copy-start.2
  92.3 6.0 %collective-permute-start.1 = (bf16[2048,128]{1,0:T(8,128)(2,1)}, bf16[2048,128]{1,0:T(8,128)(2,1)S(1)}, u32[]{:S(2)}, u32[]{:S(2)}) collective-permute-start(bf16[2048,128]{1,0:T(8,128)(2,1)} %get-tuple-element.24), channel_id=1, source_target_pairs={{0,32},{32,0},{1,33},{33,1},{2,34},{34,2},{3,35},{35,3},{4,36},{36... | collective-permute-start | bytes 1572872 | tf_op jit(solution)/shard_map/ppermute | solution.py:256
  98.4 0.8 copy-start.4
  101.8 30.6 %all-to-all-start.3 = ((bf16[128,24,128]{2,1,0:T(8,128)(2,1)}), bf16[128,24,128]{2,1,0:T(8,128)(2,1)S(1)}, u32[]{:S(2)}, u32[]{:S(2)}) async-start(bf16[128,24,128]{2,1,0:T(8,128)(2,1)} %bitcast.24), calls=%async_computation.3 | async-start | bytes 1572864 | tf_op jit(solution)/shard_map/all_to_all | solution.py:250
  132.4 0.9 copy-start.1

commit v3 on v2

v3 whole, which is shorter than its diff:
```python
import functools

import jax
import jax.numpy as jnp
from jax import lax
from jax.experimental import pallas as pl
from jax.experimental.pallas import tpu as pltpu
from jax.sharding import Mesh
from jax.sharding import PartitionSpec as P

IA = ("zl", "co")
JA = ("y", "x", "zh")
SPLIT = ("zl", "y", "x", "zh")

epsilon = 1e-05
F32 = jnp.float32
BF16 = jnp.bfloat16


ROWS = 18


def stats(values):
    centre = jnp.mean(values, axis=-1, keepdims=True)
    shifted = values - centre
    inverse = lax.rsqrt(jnp.mean(shifted * shifted, axis=-1, keepdims=True) + epsilon)
    return shifted * inverse, inverse


def norm_back(scaled, inverse, grad_out, gain):
    grad_hat = grad_out * gain
    first_mean = jnp.mean(grad_hat, axis=-1, keepdims=True)
    second_mean = jnp.mean(grad_hat * scaled, axis=-1, keepdims=True)
    return inverse * (grad_hat - first_mean - scaled * second_mean)


def dot(a, b, dims=((1,), (0,))):
    return lax.dot_general(a, b, (dims, ((), ())), preferred_element_type=F32)


def edges(rows, weights, gain, bias):
    scaled, inverse = stats(rows.astype(F32))
    hidden = dot((scaled * gain + bias).astype(BF16), weights)
    return hidden[:, :128], jax.nn.sigmoid(hidden[:, 128:]), scaled, inverse


def lane_group(shape):
    return lax.broadcasted_iota(jnp.int32, shape, 1) // 32


def moved(block, source, target):
    shift = ((target - source) * 32) % 128
    return block if shift == 0 else pltpu.roll(block, shift, 1)


def tail_k(r, g):
    return 16 + 4 * (r - 16) + g


def project_kernel(gain, bias, w_left, slab, w_right, column, out, left_rows, chunks):
    g, b = gain()[...], bias()[...]
    w_left, slab = w_left(), slab()
    for step in range(8):
        rows = pl.ds(step * 96, 96)
        linear, sigma, _, _ = edges(slab[rows, :], w_left[...], g, b)
        left_rows[rows, :] = sigma * linear

    def left_part(k):
        return left_rows[pl.ds(k, 32, stride=24), :]

    w_right, column = w_right(), column()
    for r in range(ROWS):
        if r < 16:
            linear, sigma, _, _ = edges(column[pl.ds(r * 96, 96), :], w_right[...], g, b)
            parts = [sigma * linear, left_part(r)]
        else:
            parts = [left_part(tail_k(r, q)) for q in range(4)]
        chunks[pl.ds(r, 128, stride=ROWS), :] = jnp.concatenate(parts, axis=0).T
    out[...] = chunks[...].astype(BF16)


def gathered(parts, sources, targets, group):
    merged = None
    for part, source, target in zip(parts, sources, targets):
        piece = moved(part, source, target)
        merged = piece if merged is None else jnp.where(group == target, piece, merged)
    return merged


def padded(rows):
    return jnp.concatenate([rows, jnp.zeros((32, 128), BF16)], axis=0)


def left_block(left, zl, core):
    start = pl.multiple_of((2 * zl + core) * 96, 32)
    return padded(left[pl.ds(start, 96), :])


def first_product_kernel(core, got, left, right, partial, rows, left_rows):
    group = lane_group((32, 128))
    rows[...] = got[...].astype(F32)
    for r in range(ROWS):
        parts = [rows[pl.ds(zl * 32 * ROWS + r, 32, stride=ROWS), :] for zl in range(4)]
        if r < 16:
            for zl in range(4):
                right[pl.ds(zl * 512 + r * 32, 32), :] = parts[zl].astype(BF16)
            left_rows[pl.ds(r, 32, stride=24), :] = gathered(parts, (3,) * 4, range(4), group)
        else:
            for q in range(4):
                left_rows[pl.ds(tail_k(r, q), 32, stride=24), :] = gathered(
                    parts, (q,) * 4, range(4), group
                )
    left[...] = left_rows[...].astype(BF16)
    total = None
    for zl in range(4):
        term = dot(right[pl.ds(zl * 512, 512), :], left_block(left, zl, core[0]))
        total = term if total is None else total + term
    partial[...] = total


def second_product_kernel(core, come, left, partial, right, out, rows, sent):
    rows[...] = come[...].astype(F32)
    acc = partial[...]
    for zl in range(4):
        for r in range(16):
            right[pl.ds(zl * 512 + r * 32, 32), :] = rows[
                pl.ds(zl * 32 * ROWS + r, 32, stride=ROWS), :
            ].astype(BF16)
        acc = acc + dot(right[pl.ds(zl * 512, 512), :], left_block(left, zl, 1 - core[0]))
    group = lane_group((32, 128))
    for jh in range(4):
        parts = [acc[(4 * jh + jl) * 32 : (4 * jh + jl + 1) * 32, :] for jl in range(4)]
        for zl in range(4):
            sent[pl.ds(zl * 128 + jh, 32, stride=4), :] = gathered(
                parts, (zl,) * 4, range(4), group
            )
    out[...] = sent[...].astype(BF16)


def gate_of(tile, gate_w, gain, bias):
    scaled, inverse = stats(tile[...].astype(F32))
    hidden = dot((scaled * gain[...] + bias[...]).astype(BF16), gate_w[...])
    return jax.nn.sigmoid(hidden), scaled, inverse


def gate_kernel(gain, bias, u_gain, gate_w, tile, out_w, cotangent, eg_out, rows):
    gate, _, _ = gate_of(tile(), gate_w(), gain(), bias())
    grad_outer = (cotangent()[...].astype(F32) * gate).astype(BF16)
    rows[...] = dot(grad_outer, out_w()[...], ((1,), (1,))) * u_gain()[...]
    for jh in range(4):
        block = jnp.concatenate(
            [rows[pl.ds(4 * jh + jl, 32, stride=16), :] for jl in range(4)], axis=0
        )
        eg_out[pl.ds(jh * 128, 128), :] = block.T


def tri_back_kernel(tri, eg, out, tri_rows, d_rows):
    tri_rows[...] = tri[...].astype(F32)
    for jh in range(4):
        value = tri_rows[pl.ds(jh, 128, stride=4), :]
        centre = jnp.mean(value, axis=0, keepdims=True)
        shifted = value - centre
        inverse = lax.rsqrt(jnp.mean(shifted * shifted, axis=0, keepdims=True) + epsilon)
        scaled = shifted * inverse
        grad_hat = eg[pl.ds(jh * 128, 128), :]
        first_mean = jnp.mean(grad_hat, axis=0, keepdims=True)
        second_mean = jnp.mean(grad_hat * scaled, axis=0, keepdims=True)
        d_rows[pl.ds(jh, 128, stride=4), :] = inverse * (
            grad_hat - first_mean - scaled * second_mean
        )
    out[...] = d_rows[...].astype(BF16)


def tile_kernel(
    tri, gain, bias, u_gain, u_bias, gate_w, tile, out_w, cotangent,
    update, grad_tile, mark, tri_rows, run_rows,
):
    gain, bias, gate_w = gain(), bias(), gate_w()
    mark[...] = jnp.zeros_like(mark)
    tri_rows[...] = tri[...].astype(F32)
    for jh in range(4):
        block = tri_rows[pl.ds(jh, 128, stride=4), :].T
        for jl in range(4):
            run_rows[pl.ds(4 * jh + jl, 32, stride=16), :] = block[jl * 32 : jl * 32 + 32, :]
    tri_scaled, _ = stats(run_rows[...])
    outer = dot((tri_scaled * u_gain()[...] + u_bias()[...]).astype(BF16), out_w()[...])
    gate, scaled, inverse = gate_of(tile(), gate_w, gain, bias)
    update[...] = (gate * outer).astype(BF16)
    grad_gate = (cotangent()[...].astype(F32) * outer * gate * (1.0 - gate)).astype(BF16)
    grad_norm = dot(grad_gate, gate_w[...], ((1,), (1,)))
    grad_tile[...] = norm_back(scaled, inverse, grad_norm, gain[...]).astype(BF16)


def factor_kernel(
    gain, bias, w_left, slab, w_right, column,
    kept,
):
    g, b = gain()[...], bias()[...]
    w_left, slab, w_right, column = w_left(), slab(), w_right(), column()
    for n, weights in enumerate((w_left, w_right)):
        for half in range(2):
            kept[pl.ds(9216 + (2 * n + half) * 128, 128), :] = weights[
                :, half * 128 : half * 128 + 128
            ]
    for step in range(24):
        source, weights = (slab, w_left) if step < 8 else (column, w_right)
        start = step * 96 if step < 8 else (step - 8) * 96
        linear, sigma, scaled, inverse = edges(source[pl.ds(start, 96), :], weights[...], g, b)
        values = (sigma, linear * sigma * (1.0 - sigma), inverse * g, scaled)
        for plane, value in enumerate(values):
            kept[pl.ds(plane * 2304 + step * 96, 96), :] = value.astype(BF16)


def third_product_kernel(core, d_got, left, mark, d_tri, d_right, rows, d_rows):
    group = lane_group((32, 128))
    rows[...] = d_got[...].astype(F32)
    for jh in range(4):
        parts = [rows[pl.ds(zl * 128 + jh, 32, stride=4), :] for zl in range(4)]
        for jl in range(4):
            d_rows[pl.ds((4 * jh + jl) * 32, 32), :] = gathered(parts, (jl,) * 4, range(4), group)
    d_now = d_rows[...].astype(BF16)
    d_tri[...] = d_now
    for zl in range(4):
        block = dot(d_now, left_block(left, zl, 1 - core[0]), ((1,), (1,)))
        d_right[pl.ds(zl * 512, 512), :] = block.astype(BF16)


def fourth_product_kernel(core, d_tri, right_own, right_other, left, base, d_left):
    d_now = d_tri[...]
    d_t = d_now.astype(F32).T.astype(BF16)
    for zl in range(4):
        for right, which in ((right_own, core[0]), (right_other, 1 - core[0])):
            block = dot(d_t, right[pl.ds(zl * 512, 512), :]).T
            start = pl.multiple_of((2 * zl + which) * 96, 32)
            d_left[pl.ds(start, 96), :] = block[:96, :]
    group = lane_group((32, 128))

    def left_part(k):
        return d_left[pl.ds(k, 32, stride=24), :]

    for zl in range(4):
        block = dot(d_now, left_block(left, zl, core[0]), ((1,), (1,)))
        for r in range(ROWS):
            if r < 16:
                merged = jnp.where(
                    group == 3, moved(left_part(r), zl, 3), block[r * 32 : r * 32 + 32, :]
                )
            else:
                parts = [left_part(tail_k(r, q)) for q in range(4)]
                merged = gathered(parts, (zl,) * 4, range(4), group)
            base[pl.ds(zl * 32 * ROWS + r, 32, stride=ROWS), :] = merged


def fifth_product_kernel(come, base, out, rows):
    for zl in range(4):
        for r in range(ROWS):
            target = pl.ds(zl * 32 * ROWS + r, 32, stride=ROWS)
            if r < 16:
                rows[target, :] = come[pl.ds(zl * 512 + r * 32, 32), :].astype(F32)
            else:
                rows[target, :] = jnp.zeros((32, 128), F32)
    out[...] = (base[...] + rows[...]).astype(BF16)


def edges_back(grad_edge, start, weights, kept):
    sigma, slope, scale, scaled = (
        kept[pl.ds(plane * 2304 + start, 96), :].astype(F32) for plane in range(4)
    )
    joined = jnp.concatenate([grad_edge * sigma, grad_edge * slope], axis=1)
    grad_hat = dot(joined.astype(BF16), weights, ((1,), (1,))) * scale
    first_mean = jnp.mean(grad_hat, axis=-1, keepdims=True)
    second_mean = jnp.mean(grad_hat * scaled, axis=-1, keepdims=True)
    return (grad_hat - first_mean - scaled * second_mean).astype(BF16)


def project_back_kernel(
    back, kept, grad_slab, grad_column, chunks, left_rows
):
    w_left, w_right = (
        jnp.concatenate(
            [kept[pl.ds(9216 + (2 * n + half) * 128, 128), :] for half in range(2)], axis=1
        )
        for n in range(2)
    )
    chunks[...] = back[...].astype(F32)
    for r in range(ROWS):
        block = chunks[pl.ds(r, 128, stride=ROWS), :].T
        if r < 16:
            left_rows[pl.ds(r, 32, stride=24), :] = block[96:, :]
            grad_column[pl.ds(r * 96, 96), :] = edges_back(
                block[:96, :], 768 + r * 96, w_right, kept
            )
        else:
            for q in range(4):
                left_rows[pl.ds(tail_k(r, q), 32, stride=24), :] = block[q * 32 : q * 32 + 32, :]
    for step in range(8):
        rows = pl.ds(step * 96, 96)
        grad_slab[rows, :] = edges_back(left_rows[rows, :], step * 96, w_left, kept)


VMEM = pl.BlockSpec(memory_space=pltpu.VMEM)
SMEM = pl.BlockSpec(memory_space=pltpu.SMEM)
HBM = pl.BlockSpec(memory_space=pltpu.HBM)


class Staged:
    def __init__(self, copy, ref):
        self.copy, self.ref, self.waiting = copy, ref, True
        copy.start()

    def __call__(self):
        if self.waiting:
            self.copy.wait()
            self.waiting = False
        return self.ref


def run(kernel, name, outs, scratch, args, fetched=(), limit=16, cost=2_000_000):
    cuts = [len(args), len(fetched), len(outs), len(scratch), len(fetched)]

    def body(*refs):
        groups, at = [], 0
        for size in cuts:
            groups.append(refs[at : at + size])
            at += size
        plain, sources, results, work, stages = groups
        staged = [
            Staged(pltpu.make_async_copy(source, stage, refs[-1].at[n]), stage)
            for n, (source, stage) in enumerate(zip(sources, stages))
        ]
        kernel(*plain, *staged, *results, *work)
        for item in staged:
            item()

    scratches = [pltpu.VMEM((n, 128), F32) for n in scratch]
    scratches += [pltpu.VMEM(a.shape, a.dtype) for a in fetched]
    if fetched:
        scratches.append(pltpu.SemaphoreType.DMA((len(fetched),)))
    return pl.pallas_call(
        body,
        name=name,
        out_shape=[jax.ShapeDtypeStruct(s, t) for s, t in outs],
        in_specs=[SMEM if a.dtype == jnp.int32 else VMEM for a in args] + [HBM] * len(fetched),
        out_specs=[VMEM] * len(outs),
        scratch_shapes=scratches,
        cost_estimate=pl.CostEstimate(flops=50 * cost, bytes_accessed=cost, transcendentals=0),
        compiler_params=pltpu.CompilerParams(vmem_limit_bytes=limit and limit << 20),
    )(*args, *[pltpu.with_memory_space_constraint(a, pltpu.HBM) for a in fetched])


def shuffled(array):
    rows = array.shape[0] // 128
    shape = (128, rows // 2, 2, 128) if rows == ROWS else (128, rows, 128)
    return lax.all_to_all(array.reshape(shape), SPLIT, 0, 0, tiled=True).reshape(array.shape)


def swapped(array):
    return lax.ppermute(array, "co", [(0, 1), (1, 0)])


def shards(
    slab_rows,
    column_rows,
    pair_tile,
    cotangent,
    weights_left,
    weights_right,
    gate_weight,
    out_weight,
    input_gain,
    input_bias,
    update_gain,
    update_bias,
):
    core = lax.axis_index("co").astype(jnp.int32).reshape(1)
    slab = slab_rows.reshape(768, 128)
    column = column_rows.reshape(1536, 128)
    tile = pair_tile.reshape(512, 128)
    cots = cotangent.reshape(512, 128)
    gain, bias, u_gain, u_bias = (
        v.reshape(1, 128) for v in (input_gain, input_bias, update_gain, update_bias)
    )
    (sent,) = run(
        project_kernel, "project", [((128 * ROWS, 128), BF16)], [768, 128 * ROWS], (),
        (gain, bias, weights_left, slab, weights_right, column), limit=16,
    )
    got = shuffled(sent)
    (eg,) = run(
        gate_kernel, "gate", [((512, 128), F32)], [512], (),
        (gain, bias, u_gain, gate_weight, tile, out_weight, cots),
    )
    come = swapped(got)
    left, right_own, partial = run(
        first_product_kernel, "product_one",
        [((768, 128), BF16), ((2048, 128), BF16), ((512, 128), F32)],
        [128 * ROWS, 768], (core, got),
    )
    right_other, tri_sent = run(
        second_product_kernel, "product_two",
        [((2048, 128), BF16), ((512, 128), BF16)], [128 * ROWS, 512], (core, come, left, partial),
    )
    tri = shuffled(tri_sent)
    (d_sent,) = run(tri_back_kernel, "tri_back", [((512, 128), BF16)], [512, 512], (tri, eg))
    d_got = shuffled(d_sent)
    update, grad_tile, mark = run(
        tile_kernel, "tile", [((512, 128), BF16)] * 2 + [((8, 128), F32)], [512, 512], (tri,),
        (gain, bias, u_gain, u_bias, gate_weight, tile, out_weight, cots),
    )
    d_tri, d_right_other = run(
        third_product_kernel, "product_three",
        [((512, 128), BF16), ((2048, 128), BF16)], [512, 512], (core, d_got, left, mark),
    )
    d_right_come = swapped(d_right_other)
    (base,) = run(
        fourth_product_kernel, "product_four", [((128 * ROWS, 128), F32)], [768],
        (core, d_tri, right_own, right_other, left),
    )
    (back_sent,) = run(
        fifth_product_kernel, "product_five", [((128 * ROWS, 128), BF16)], [128 * ROWS],
        (d_right_come, base),
    )
    back = shuffled(back_sent)
    (kept,) = run(
        factor_kernel, "factors",
        [((4 * 2304 + 512, 128), BF16)],
        [], (), (gain, bias, weights_left, slab, weights_right, column),
    )
    grad_slab, grad_column = run(
        project_back_kernel, "project_back",
        [((768, 128), BF16), ((1536, 128), BF16)], [128 * ROWS, 768], (back, kept),
    )
    return (
        update.reshape(pair_tile.shape),
        grad_slab.reshape(slab_rows.shape),
        grad_column.reshape(column_rows.shape),
        grad_tile.reshape(pair_tile.shape),
    )


def solution(mesh):
    finer = Mesh(mesh.devices.reshape(4, 2, 4, 4, 2), ("zl", "co", "y", "x", "zh"))
    row_spec = P(IA, JA, None)
    column_spec = P(JA, IA, None)
    in_specs = (row_spec, column_spec, row_spec, row_spec) + (P(),) * 8
    return jax.shard_map(
        shards,
        mesh=finer,
        in_specs=in_specs,
        out_specs=(row_spec, row_spec, column_spec, row_spec),
        check_vma=False,
    )
```

time: 139 us -> 113 us (0.81)
  blocking collectives: 57 us -> 35 us
  Pallas kernels: 28.3 us -> 17.3 us
  starting transfers between devices: 19.5 us -> 25.6 us
  waiting for transfers between devices: 29.5 us -> 33.8 us
  local copies, waits for them, and re-layouts: 3.27 us -> 0 us
    all_to_all x2 -> x1, blocking collectives: 57 us -> 35 us  [shuffled(): lax.all_to_all(array.reshape(shape), SPLIT, 0, 0, tiled=True)]
    pallas_call x10 -> x11, Pallas kernels: 28.3 us -> 17.3 us  [run(): pl.pallas_call(body, name=name, out_shape=[jax.ShapeDtypeStruct(s, t) for...]
    all_to_all x2 -> x3, starting transfers between devices: 12.9 us -> 19.7 us  [shuffled(): lax.all_to_all(array.reshape(shape), SPLIT, 0, 0, tiled=True)]
    unnamed x10 -> x0, local copies, waits for them, and re-layouts: 3.27 us -> none
    all_to_all x2 -> x3, waiting for transfers between devices: 29.5 us -> 32.3 us  [shuffled(): lax.all_to_all(array.reshape(shape), SPLIT, 0, 0, tiled=True)]
    ppermute x2, waiting for transfers between devices: 0.01 us -> 1.6 us  [swapped(): return lax.ppermute(array, 'co', [(0, 1), (1, 0)])]
  transfers between devices with their start and end apart: 4 -> 5, of which waited for: 2 -> 5; matrix products, arithmetic and copies ran while one was open for 0% -> 0% of each run, Pallas kernels for 7% -> 8%
where the time goes in v3:
time: 113 us; the launch traced here: 112 us
  blocking collectives  35 us (31%)
  waiting for transfers between devices  33.8 us (30%)
  starting transfers between devices  25.6 us (23%)
  Pallas kernels  17.3 us (15%)
    all_to_all x1, blocking collectives, shuffled(): lax.all_to_all(array.reshape(shape), SPLIT, 0, 0, tiled=True)  35 us
    all_to_all x3, waiting for transfers between devices, shuffled(): lax.all_to_all(array.reshape(shape), SPLIT, 0, 0, tiled=True)  32.3 us
    all_to_all x3, starting transfers between devices, shuffled(): lax.all_to_all(array.reshape(shape), SPLIT, 0, 0, tiled=True)  19.7 us
    pallas_call x11, Pallas kernels, run(): pl.pallas_call(body, name=name, out_shape=[jax.ShapeDtypeStruct(s, t) for...  17.3 us
    ppermute x2, starting transfers between devices, swapped(): return lax.ppermute(array, 'co', [(0, 1), (1, 0)])  5.9 us
  transfers between devices with their start and end apart: 5, of which 5 were waited for; matrix products, arithmetic and copies ran while one was open for 0% of the time, Pallas kernels for 8%

profile of v3, /device:TPU:1, one launch (start us, length us, event | category | flops | bytes accessed | tf_op | source)
XLA Modules:
  0.0 112.5 jit_solution(16719488610539693492)
XLA Ops:
  0.6 3.1 %project.1 = bf16[2304,128]{1,0:T(8,128)(2,1)S(1)} custom-call(f32[1,128]{1,0:T(1,128)} %bitcast.36, f32[1,128]{1,0:T(1,128)} %bitcast.40, bf16[128,256]{1,0:T(8,128)(2,1)} %refs_2_.3, bf16[768,128]{1,0:T(8,128)(2,1)} %bitcast.30, bf16[128,256]{1,0:T(8,128)(2,1)} %refs_4_.3, bf16[1536,128]{1,0:T(8,128)(2,1)} %bitcast.28), custom_call_target="tpu_custom_call" | custom-call | flops 100000000 | bytes 2000000 | tf_op jit(solution)/shard_map/project/pallas_call | solution.py:339
  3.7 35.0 %all_to_all.20 = bf16[128,9,2,128]{3,2,1,0:T(2,128)(2,1)S(1)} all-to-all(bf16[128,9,2,128]{3,2,1,0:T(2,128)(2,1)S(1)} %bitcast.23), channel_id=1, replica_groups=mesh['zl'=4,'co'=2,'y'=4,'x'=4,'zh'=2] {'zl','y','x','zh'}, dimensions={0} | all-to-all | bytes 1179648 | tf_op jit(solution)/shard_map/all_to_all | solution.py:354
  38.7 3.0 %collective-permute-start = (bf16[2304,128]{1,0:T(8,128)(2,1)S(1)}, bf16[2304,128]{1,0:T(8,128)(2,1)S(1)}, u32[]{:S(2)}, u32[]{:S(2)}) collective-permute-start(bf16[2304,128]{1,0:T(8,128)(2,1)S(1)} %bitcast.21), channel_id=1, source_target_pairs={{0,32},{32,0},{1,33},{33,1},{2,34},{34,2},{3,35},{35,3},{4,36},{36... | collective-permute-start | bytes 1769480 | tf_op jit(solution)/shard_map/ppermute | solution.py:358
  41.7 0.6 product_one.1
  42.3 1.0 collective-permute-done.refs_1_
  43.3 1.2 %product_two.1 = (bf16[2048,128]{1,0:T(8,128)(2,1)S(1)}, bf16[512,128]{1,0:T(8,128)(2,1)}) custom-call(s32[1]{0:T(128)} %bitcast.refs_0_, bf16[2304,128]{1,0:T(8,128)(2,1)S(1)} %collective-permute-done.refs_1_, bf16[768,128]{1,0:T(8,128)(2,1)S(1)} %get-tuple-element.16.refs_2_.refs_4_, f32[512,128]{1,0:T(8,128)S(1)} %get-tuple-element.17.refs_3_), custom_call_target="tpu_custom_call" | custom-call | flops 100000000 | bytes 2000000 | tf_op jit(solution)/shard_map/product_two/pallas_call | solution.py:339
  44.6 6.5 %all-to-all-start.1 = ((bf16[128,4,128]{2,1,0:T(4,128)(2,1)}), bf16[128,4,128]{2,1,0:T(4,128)(2,1)S(1)}, u32[]{:S(2)}, u32[]{:S(2)}) async-start(bf16[128,4,128]{2,1,0:T(4,128)(2,1)} %bitcast.7), calls=%async_computation.1 | async-start | bytes 262144 | tf_op jit(solution)/shard_map/all_to_all | solution.py:354
  51.1 1.8 %gate.1.refs_1_ = f32[512,128]{1,0:T(8,128)S(1)} custom-call(f32[1,128]{1,0:T(1,128)} %bitcast.37, f32[1,128]{1,0:T(1,128)} %bitcast.41, f32[1,128]{1,0:T(1,128)} %bitcast.44, bf16[128,128]{1,0:T(8,128)(2,1)} %refs_3_.1, bf16[512,128]{1,0:T(8,128)(2,1)} %bitcast.32, bf16[128,128]{1,0:T(8,128)(2,1)} %refs_5_.3, bf16[512,128]{1,0:T(8,128)(2,1)} %bitcast.34), custom_call_target="tpu_custom_call" | custom-call | flops 100000000 | bytes 2000000 | tf_op jit(solution)/shard_map/gate/pallas_call | solution.py:339
  52.9 8.4 %all-to-all-done.1 = bf16[128,4,128]{2,1,0:T(4,128)(2,1)S(1)} async-done(((bf16[128,4,128]{2,1,0:T(4,128)(2,1)}), bf16[128,4,128]{2,1,0:T(4,128)(2,1)S(1)}, u32[]{:S(2)}, u32[]{:S(2)}) %all-to-all-start.1) | async-done | bytes 131104 | tf_op jit(solution)/shard_map/all_to_all | solution.py:354
  61.3 0.9 tri_back.1
  62.2 7.1 %all-to-all-start.2 = ((bf16[128,4,128]{2,1,0:T(4,128)(2,1)}), bf16[128,4,128]{2,1,0:T(4,128)(2,1)S(1)}, u32[]{:S(2)}, u32[]{:S(2)}) async-start(bf16[128,4,128]{2,1,0:T(4,128)(2,1)} %bitcast.14), calls=%async_computation.2 | async-start | bytes 262144 | tf_op jit(solution)/shard_map/all_to_all | solution.py:354
  69.3 2.9 %tile.1 = (bf16[512,128]{1,0:T(8,128)(2,1)}, bf16[512,128]{1,0:T(8,128)(2,1)}, f32[8,128]{1,0:T(8,128)S(1)}) custom-call(bf16[512,128]{1,0:T(8,128)(2,1)S(1)} %bitcast.26, f32[1,128]{1,0:T(1,128)} %bitcast.38, f32[1,128]{1,0:T(1,128)} %bitcast.42, f32[1,128]{1,0:T(1,128)} %bitcast.45, f32[1,128]{1,0:T(1,128)} %bitcast.46, bf16[128,128]{1,0:T(8,128)(2,1)} %refs_3_.1, ...), custom_call_target="tpu_custom_call" | custom-call | flops 100000000 | bytes 2000000 | tf_op jit(solution)/shard_map/tile/pallas_call | solution.py:339
  72.2 7.3 %all-to-all-done.2 = bf16[128,4,128]{2,1,0:T(4,128)(2,1)S(1)} async-done(((bf16[128,4,128]{2,1,0:T(4,128)(2,1)}), bf16[128,4,128]{2,1,0:T(4,128)(2,1)S(1)}, u32[]{:S(2)}, u32[]{:S(2)}) %all-to-all-start.2) | async-done | bytes 131104 | tf_op jit(solution)/shard_map/all_to_all | solution.py:354
  79.5 0.4 product_three.1
  79.9 2.9 %collective-permute-start.1 = (bf16[2048,128]{1,0:T(8,128)(2,1)S(1)}, bf16[2048,128]{1,0:T(8,128)(2,1)S(1)}, u32[]{:S(2)}, u32[]{:S(2)}) collective-permute-start(bf16[2048,128]{1,0:T(8,128)(2,1)S(1)} %get-tuple-element.21), channel_id=1, source_target_pairs={{0,32},{32,0},{1,33},{33,1},{2,34},{34,2},{3,35},{35,3},{4,36},{36... | collective-permute-start | bytes 1572872 | tf_op jit(solution)/shard_map/ppermute | solution.py:358
  82.8 0.9 product_four.1.refs_1_
  83.7 0.6 collective-permute-done.1.refs_0_
  84.3 1.0 product_five.1
  85.4 6.2 %all-to-all-start.3 = ((bf16[128,9,2,128]{3,2,1,0:T(2,128)(2,1)}), bf16[128,9,2,128]{3,2,1,0:T(2,128)(2,1)S(1)}, u32[]{:S(2)}, u32[]{:S(2)}) async-start(bf16[128,9,2,128]{3,2,1,0:T(2,128)(2,1)} %bitcast.16), calls=%async_computation.3 | async-start | bytes 1179648 | tf_op jit(solution)/shard_map/all_to_all | solution.py:354
  91.6 2.6 %factors.1.refs_1_ = bf16[9728,128]{1,0:T(8,128)(2,1)S(1)} custom-call(f32[1,128]{1,0:T(1,128)} %bitcast.39, f32[1,128]{1,0:T(1,128)} %bitcast.43, bf16[128,256]{1,0:T(8,128)(2,1)} %refs_2_.3, bf16[768,128]{1,0:T(8,128)(2,1)} %bitcast.31, bf16[128,256]{1,0:T(8,128)(2,1)} %refs_4_.3, bf16[1536,128]{1,0:T(8,128)(2,1)} %bitcast.29), custom_call_target="tpu_custom_call" | custom-call | flops 100000000 | bytes 2000000 | tf_op jit(solution)/shard_map/factors/pallas_call | solution.py:339
  94.1 16.5 %all-to-all-done.3 = bf16[128,9,2,128]{3,2,1,0:T(2,128)(2,1)S(1)} async-done(((bf16[128,9,2,128]{3,2,1,0:T(2,128)(2,1)}), bf16[128,9,2,128]{3,2,1,0:T(2,128)(2,1)S(1)}, u32[]{:S(2)}, u32[]{:S(2)}) %all-to-all-start.3) | async-done | bytes 589856 | tf_op jit(solution)/shard_map/all_to_all | solution.py:354
  110.7 1.8 %project_back.1 = (bf16[768,128]{1,0:T(8,128)(2,1)}, bf16[1536,128]{1,0:T(8,128)(2,1)}) custom-call(bf16[2304,128]{1,0:T(8,128)(2,1)S(1)} %bitcast.24, bf16[9728,128]{1,0:T(8,128)(2,1)S(1)} %factors.1.refs_1_), custom_call_target="tpu_custom_call" | custom-call | flops 100000000 | bytes 2000000 | tf_op jit(solution)/shard_map/project_back/pallas_call | solution.py:339
Async XLA Ops:
  38.7 4.6 %collective-permute-start = (bf16[2304,128]{1,0:T(8,128)(2,1)S(1)}, bf16[2304,128]{1,0:T(8,128)(2,1)S(1)}, u32[]{:S(2)}, u32[]{:S(2)}) collective-permute-start(bf16[2304,128]{1,0:T(8,128)(2,1)S(1)} %bitcast.21), channel_id=1, source_target_pairs={{0,32},{32,0},{1,33},{33,1},{2,34},{34,2},{3,35},{35,3},{4,36},{36... | collective-permute-start | bytes 1769480 | tf_op jit(solution)/shard_map/ppermute | solution.py:358
  44.6 16.7 %all-to-all-start.1 = ((bf16[128,4,128]{2,1,0:T(4,128)(2,1)}), bf16[128,4,128]{2,1,0:T(4,128)(2,1)S(1)}, u32[]{:S(2)}, u32[]{:S(2)}) async-start(bf16[128,4,128]{2,1,0:T(4,128)(2,1)} %bitcast.7), calls=%async_computation.1 | async-start | bytes 262144 | tf_op jit(solution)/shard_map/all_to_all | solution.py:354
  62.2 17.3 %all-to-all-start.2 = ((bf16[128,4,128]{2,1,0:T(4,128)(2,1)}), bf16[128,4,128]{2,1,0:T(4,128)(2,1)S(1)}, u32[]{:S(2)}, u32[]{:S(2)}) async-start(bf16[128,4,128]{2,1,0:T(4,128)(2,1)} %bitcast.14), calls=%async_computation.2 | async-start | bytes 262144 | tf_op jit(solution)/shard_map/all_to_all | solution.py:354
  79.9 4.4 %collective-permute-start.1 = (bf16[2048,128]{1,0:T(8,128)(2,1)S(1)}, bf16[2048,128]{1,0:T(8,128)(2,1)S(1)}, u32[]{:S(2)}, u32[]{:S(2)}) collective-permute-start(bf16[2048,128]{1,0:T(8,128)(2,1)S(1)} %get-tuple-element.21), channel_id=1, source_target_pairs={{0,32},{32,0},{1,33},{33,1},{2,34},{34,2},{3,35},{35,3},{4,36},{36... | collective-permute-start | bytes 1572872 | tf_op jit(solution)/shard_map/ppermute | solution.py:358
  85.4 25.3 %all-to-all-start.3 = ((bf16[128,9,2,128]{3,2,1,0:T(2,128)(2,1)}), bf16[128,9,2,128]{3,2,1,0:T(2,128)(2,1)S(1)}, u32[]{:S(2)}, u32[]{:S(2)}) async-start(bf16[128,9,2,128]{3,2,1,0:T(2,128)(2,1)} %bitcast.16), calls=%async_computation.3 | async-start | bytes 1179648 | tf_op jit(solution)/shard_map/all_to_all | solution.py:354

commit v4 on v3

--- a/solution.py
+++ b/solution.py
@@ -18,6 +18,7 @@
 
 
 ROWS = 18
+SPAN = 384
 
 
 def stats(values):
@@ -60,8 +61,8 @@
 def project_kernel(gain, bias, w_left, slab, w_right, column, out, left_rows, chunks):
     g, b = gain()[...], bias()[...]
     w_left, slab = w_left(), slab()
-    for step in range(8):
-        rows = pl.ds(step * 96, 96)
+    for step in range(768 // SPAN):
+        rows = pl.ds(step * SPAN, SPAN)
         linear, sigma, _, _ = edges(slab[rows, :], w_left[...], g, b)
         left_rows[rows, :] = sigma * linear
 
@@ -69,10 +70,14 @@
         return left_rows[pl.ds(k, 32, stride=24), :]
 
     w_right, column = w_right(), column()
+    values = None
     for r in range(ROWS):
         if r < 16:
-            linear, sigma, _, _ = edges(column[pl.ds(r * 96, 96), :], w_right[...], g, b)
-            parts = [sigma * linear, left_part(r)]
+            at = r * 96 % SPAN
+            if at == 0:
+                linear, sigma, _, _ = edges(column[pl.ds(r * 96, SPAN), :], w_right[...], g, b)
+                values = sigma * linear
+            parts = [values[at : at + 96, :], left_part(r)]
         else:
             parts = [left_part(tail_k(r, q)) for q in range(4)]
         chunks[pl.ds(r, 128, stride=ROWS), :] = jnp.concatenate(parts, axis=0).T
@@ -99,17 +104,12 @@
 def first_product_kernel(core, got, left, right, partial, rows, left_rows):
     group = lane_group((32, 128))
     rows[...] = got[...].astype(F32)
-    for r in range(ROWS):
-        parts = [rows[pl.ds(zl * 32 * ROWS + r, 32, stride=ROWS), :] for zl in range(4)]
-        if r < 16:
-            for zl in range(4):
-                right[pl.ds(zl * 512 + r * 32, 32), :] = parts[zl].astype(BF16)
-            left_rows[pl.ds(r, 32, stride=24), :] = gathered(parts, (3,) * 4, range(4), group)
-        else:
-            for q in range(4):
-                left_rows[pl.ds(tail_k(r, q), 32, stride=24), :] = gathered(
-                    parts, (q,) * 4, range(4), group
-                )
+    left_of(rows, left_rows, group)
+    for zl in range(4):
+        for r in range(16):
+            right[pl.ds(zl * 512 + r * 32, 32), :] = rows[
+                pl.ds(zl * 32 * ROWS + r, 32, stride=ROWS), :
+            ].astype(BF16)
     left[...] = left_rows[...].astype(BF16)
     total = None
     for zl in range(4):
@@ -118,7 +118,7 @@
     partial[...] = total
 
 
-def second_product_kernel(core, come, left, partial, right, out, rows, sent):
+def second_product_kernel(core, come, left, partial, mark, right, out, rows, sent):
     rows[...] = come[...].astype(F32)
     acc = partial[...]
     for zl in range(4):
@@ -144,9 +144,9 @@
 
 
 def gate_kernel(gain, bias, u_gain, gate_w, tile, out_w, cotangent, eg_out, rows):
-    gate, _, _ = gate_of(tile(), gate_w(), gain(), bias())
-    grad_outer = (cotangent()[...].astype(F32) * gate).astype(BF16)
-    rows[...] = dot(grad_outer, out_w()[...], ((1,), (1,))) * u_gain()[...]
+    gate, _, _ = gate_of(tile, gate_w, gain, bias)
+    grad_outer = (cotangent[...].astype(F32) * gate).astype(BF16)
+    rows[...] = dot(grad_outer, out_w[...], ((1,), (1,))) * u_gain[...]
     for jh in range(4):
         block = jnp.concatenate(
             [rows[pl.ds(4 * jh + jl, 32, stride=16), :] for jl in range(4)], axis=0
@@ -173,10 +173,9 @@
 
 def tile_kernel(
     tri, gain, bias, u_gain, u_bias, gate_w, tile, out_w, cotangent,
-    update, grad_tile, mark, tri_rows, run_rows,
+    update, grad_tile, tri_rows, run_rows,
 ):
     gain, bias, gate_w = gain(), bias(), gate_w()
-    mark[...] = jnp.zeros_like(mark)
     tri_rows[...] = tri[...].astype(F32)
     for jh in range(4):
         block = tri_rows[pl.ds(jh, 128, stride=4), :].T
@@ -211,29 +210,35 @@
             kept[pl.ds(plane * 2304 + step * 96, 96), :] = value.astype(BF16)
 
 
-def third_product_kernel(core, d_got, left, mark, d_tri, d_right, rows, d_rows):
-    group = lane_group((32, 128))
-    rows[...] = d_got[...].astype(F32)
+def left_of(rows, left_rows, group):
+    for r in range(ROWS):
+        parts = [rows[pl.ds(zl * 32 * ROWS + r, 32, stride=ROWS), :] for zl in range(4)]
+        for q in (3,) if r < 16 else range(4):
+            k = r if r < 16 else tail_k(r, q)
+            left_rows[pl.ds(k, 32, stride=24), :] = gathered(parts, (q,) * 4, range(4), group)
+
+
+def tri_of(got, rows, d_rows, group):
+    rows[...] = got[...].astype(F32)
     for jh in range(4):
         parts = [rows[pl.ds(zl * 128 + jh, 32, stride=4), :] for zl in range(4)]
         for jl in range(4):
             d_rows[pl.ds((4 * jh + jl) * 32, 32), :] = gathered(parts, (jl,) * 4, range(4), group)
-    d_now = d_rows[...].astype(BF16)
-    d_tri[...] = d_now
-    for zl in range(4):
-        block = dot(d_now, left_block(left, zl, 1 - core[0]), ((1,), (1,)))
-        d_right[pl.ds(zl * 512, 512), :] = block.astype(BF16)
-
-
-def fourth_product_kernel(core, d_tri, right_own, right_other, left, base, d_left):
-    d_now = d_tri[...]
-    d_t = d_now.astype(F32).T.astype(BF16)
+    return d_rows[...].astype(BF16)
+
+
+def third_product_kernel(
+    core, d_got, left, come, right_own, right_other,
+    base, left_come, rows, d_rows, d_left, come_rows, left_rows,
+):
+    group = lane_group((32, 128))
+    d_now = tri_of(d_got, rows, d_rows, group)
+    d_t = d_rows[...].T.astype(BF16)
     for zl in range(4):
         for right, which in ((right_own, core[0]), (right_other, 1 - core[0])):
             block = dot(d_t, right[pl.ds(zl * 512, 512), :]).T
             start = pl.multiple_of((2 * zl + which) * 96, 32)
             d_left[pl.ds(start, 96), :] = block[:96, :]
-    group = lane_group((32, 128))
 
     def left_part(k):
         return d_left[pl.ds(k, 32, stride=24), :]
@@ -249,22 +254,28 @@
                 parts = [left_part(tail_k(r, q)) for q in range(4)]
                 merged = gathered(parts, (zl,) * 4, range(4), group)
             base[pl.ds(zl * 32 * ROWS + r, 32, stride=ROWS), :] = merged
-
-
-def fifth_product_kernel(come, base, out, rows):
-    for zl in range(4):
+    come_rows[...] = come[...].astype(F32)
+    left_of(come_rows, left_rows, group)
+    left_come[...] = left_rows[...].astype(BF16)
+
+
+def fourth_product_kernel(core, d_come, left_come, base, out, rows, d_rows, sent):
+    group = lane_group((32, 128))
+    d_now = tri_of(d_come, rows, d_rows, group)
+    for zl in range(4):
+        block = dot(d_now, left_block(left_come, zl, core[0]), ((1,), (1,)))
         for r in range(ROWS):
             target = pl.ds(zl * 32 * ROWS + r, 32, stride=ROWS)
             if r < 16:
-                rows[target, :] = come[pl.ds(zl * 512 + r * 32, 32), :].astype(F32)
+                sent[target, :] = base[target, :] + block[r * 32 : r * 32 + 32, :]
             else:
-                rows[target, :] = jnp.zeros((32, 128), F32)
-    out[...] = (base[...] + rows[...]).astype(BF16)
+                sent[target, :] = base[target, :]
+    out[...] = sent[...].astype(BF16)
 
 
 def edges_back(grad_edge, start, weights, kept):
     sigma, slope, scale, scaled = (
-        kept[pl.ds(plane * 2304 + start, 96), :].astype(F32) for plane in range(4)
+        kept[pl.ds(plane * 2304 + start, SPAN), :].astype(F32) for plane in range(4)
     )
     joined = jnp.concatenate([grad_edge * sigma, grad_edge * slope], axis=1)
     grad_hat = dot(joined.astype(BF16), weights, ((1,), (1,))) * scale
@@ -283,19 +294,24 @@
         for n in range(2)
     )
     chunks[...] = back[...].astype(F32)
+    held = []
     for r in range(ROWS):
         block = chunks[pl.ds(r, 128, stride=ROWS), :].T
         if r < 16:
             left_rows[pl.ds(r, 32, stride=24), :] = block[96:, :]
-            grad_column[pl.ds(r * 96, 96), :] = edges_back(
-                block[:96, :], 768 + r * 96, w_right, kept
-            )
+            held.append(block[:96, :])
+            if len(held) * 96 == SPAN:
+                start = (r + 1) * 96 - SPAN
+                grad_column[pl.ds(start, SPAN), :] = edges_back(
+                    jnp.concatenate(held, axis=0), 768 + start, w_right, kept
+                )
+                held = []
         else:
             for q in range(4):
                 left_rows[pl.ds(tail_k(r, q), 32, stride=24), :] = block[q * 32 : q * 32 + 32, :]
-    for step in range(8):
-        rows = pl.ds(step * 96, 96)
-        grad_slab[rows, :] = edges_back(left_rows[rows, :], step * 96, w_left, kept)
+    for step in range(768 // SPAN):
+        rows = pl.ds(step * SPAN, SPAN)
+        grad_slab[rows, :] = edges_back(left_rows[rows, :], step * SPAN, w_left, kept)
 
 
 VMEM = pl.BlockSpec(memory_space=pltpu.VMEM)
@@ -386,7 +402,7 @@
     )
     got = shuffled(sent)
     (eg,) = run(
-        gate_kernel, "gate", [((512, 128), F32)], [512], (),
+        gate_kernel, "gate", [((512, 128), F32)], [512],
         (gain, bias, u_gain, gate_weight, tile, out_weight, cots),
     )
     come = swapped(got)
@@ -397,27 +413,24 @@
     )
     right_other, tri_sent = run(
         second_product_kernel, "product_two",
-        [((2048, 128), BF16), ((512, 128), BF16)], [128 * ROWS, 512], (core, come, left, partial),
+        [((2048, 128), BF16), ((512, 128), BF16)], [128 * ROWS, 512], (core, come, left, partial, eg),
     )
     tri = shuffled(tri_sent)
     (d_sent,) = run(tri_back_kernel, "tri_back", [((512, 128), BF16)], [512, 512], (tri, eg))
     d_got = shuffled(d_sent)
-    update, grad_tile, mark = run(
-        tile_kernel, "tile", [((512, 128), BF16)] * 2 + [((8, 128), F32)], [512, 512], (tri,),
+    update, grad_tile = run(
+        tile_kernel, "tile", [((512, 128), BF16)] * 2, [512, 512], (tri,),
         (gain, bias, u_gain, u_bias, gate_weight, tile, out_weight, cots),
     )
-    d_tri, d_right_other = run(
+    d_come = swapped(d_got)
+    base, left_come = run(
         third_product_kernel, "product_three",
-        [((512, 128), BF16), ((2048, 128), BF16)], [512, 512], (core, d_got, left, mark),
-    )
-    d_right_come = swapped(d_right_other)
-    (base,) = run(
-        fourth_product_kernel, "product_four", [((128 * ROWS, 128), F32)], [768],
-        (core, d_tri, right_own, right_other, left),
+        [((128 * ROWS, 128), F32), ((768, 128), BF16)], [512, 512, 768, 128 * ROWS, 768],
+        (core, d_got, left, come, right_own, right_other),
     )
     (back_sent,) = run(
-        fifth_product_kernel, "product_five", [((128 * ROWS, 128), BF16)], [128 * ROWS],
-        (d_right_come, base),
+        fourth_product_kernel, "product_four", [((128 * ROWS, 128), BF16)],
+        [512, 512, 128 * ROWS], (core, d_come, left_come, base),
     )
     back = shuffled(back_sent)
     (kept,) = run(

time: 113 us -> 111 us (0.982)
  blocking collectives: 35 us -> 68.8 us
  waiting for transfers between devices: 33.8 us -> 14.7 us
  starting transfers between devices: 25.6 us -> 12.1 us
  Pallas kernels: 17.3 us -> 14.5 us
    all_to_all x1 -> x3, blocking collectives: 35 us -> 68.8 us  [shuffled(): lax.all_to_all(array.reshape(shape), SPLIT, 0, 0, tiled=True)]
    all_to_all x3 -> x1, waiting for transfers between devices: 32.3 us -> 14.3 us  [shuffled(): lax.all_to_all(array.reshape(shape), SPLIT, 0, 0, tiled=True)]
    all_to_all x3 -> x1, starting transfers between devices: 19.7 us -> 6.36 us  [shuffled(): lax.all_to_all(array.reshape(shape), SPLIT, 0, 0, tiled=True)]
    pallas_call x11 -> x10, Pallas kernels: 17.3 us -> 14.5 us  [run(): pl.pallas_call(body, name=name, out_shape=[jax.ShapeDtypeStruct(s, t) for...]
    ppermute x2, waiting for transfers between devices: 1.6 us -> 0.31 us  [swapped(): return lax.ppermute(array, 'co', [(0, 1), (1, 0)])]
  transfers between devices with their start and end apart: 5 -> 3, of which waited for: 5 -> 2; matrix products, arithmetic and copies ran while one was open for 0% -> 0% of each run, Pallas kernels for 8% -> 7%
where the time goes in v4:
time: 111 us
  blocking collectives  68.8 us (62%)
  waiting for transfers between devices  14.7 us (13%)
  Pallas kernels  14.5 us (13%)
  starting transfers between devices  12.1 us (11%)
    all_to_all x3, blocking collectives, shuffled(): lax.all_to_all(array.reshape(shape), SPLIT, 0, 0, tiled=True)  68.8 us
    pallas_call x10, Pallas kernels, run(): pl.pallas_call(body, name=name, out_shape=[jax.ShapeDtypeStruct(s, t) for...  14.5 us
    all_to_all x1, waiting for transfers between devices, shuffled(): lax.all_to_all(array.reshape(shape), SPLIT, 0, 0, tiled=True)  14.3 us
    all_to_all x1, starting transfers between devices, shuffled(): lax.all_to_all(array.reshape(shape), SPLIT, 0, 0, tiled=True)  6.36 us
    ppermute x2, starting transfers between devices, swapped(): return lax.ppermute(array, 'co', [(0, 1), (1, 0)])  5.71 us
  transfers between devices with their start and end apart: 3, of which 2 were waited for; matrix products, arithmetic and copies ran while one was open for 0% of the time, Pallas kernels for 7%

profile of v4, /device:TPU:1, one launch (start us, length us, event | category | flops | bytes accessed | tf_op | source)
XLA Modules:
  0.0 110.9 jit_solution(7056500051046903555)
XLA Ops:
  0.6 0.0 copy-start.4
  0.6 0.0 copy-start.5
  0.7 0.0 copy-start.6
  0.7 0.0 copy-start
  0.7 0.0 copy-start.1
  0.7 0.0 copy-start.2
  0.7 0.0 copy-start.3
  0.7 2.7 %project.1 = bf16[2304,128]{1,0:T(8,128)(2,1)S(1)} custom-call(f32[1,128]{1,0:T(1,128)} %bitcast.35, f32[1,128]{1,0:T(1,128)} %bitcast.39, bf16[128,256]{1,0:T(8,128)(2,1)} %refs_2_.3, bf16[768,128]{1,0:T(8,128)(2,1)} %bitcast.47, bf16[128,256]{1,0:T(8,128)(2,1)} %refs_4_.3, bf16[1536,128]{1,0:T(8,128)(2,1)} %bitcast.45), custom_call_target="tpu_custom_call" | custom-call | flops 100000000 | bytes 2000000 | tf_op jit(solution)/shard_map/project/pallas_call | solution.py:355
  3.4 35.0 %all_to_all.20 = bf16[128,9,2,128]{3,2,1,0:T(2,128)(2,1)S(1)} all-to-all(bf16[128,9,2,128]{3,2,1,0:T(2,128)(2,1)S(1)} %bitcast.23), channel_id=1, replica_groups=mesh['zl'=4,'co'=2,'y'=4,'x'=4,'zh'=2] {'zl','y','x','zh'}, dimensions={0} | all-to-all | bytes 1179648 | tf_op jit(solution)/shard_map/all_to_all | solution.py:370
  38.4 3.0 %collective-permute-start = (bf16[2304,128]{1,0:T(8,128)(2,1)S(1)}, bf16[2304,128]{1,0:T(8,128)(2,1)S(1)}, u32[]{:S(2)}, u32[]{:S(2)}) collective-permute-start(bf16[2304,128]{1,0:T(8,128)(2,1)S(1)} %bitcast.21), channel_id=1, source_target_pairs={{0,32},{32,0},{1,33},{33,1},{2,34},{34,2},{3,35},{35,3},{4,36},{36... | collective-permute-start | bytes 1769480 | tf_op jit(solution)/shard_map/ppermute | solution.py:374
  41.4 0.0 copy-done.4
  41.4 0.0 copy-done.5
  41.4 0.0 copy-done.6
  41.4 0.0 copy-done
  41.4 0.0 copy-done.1
  41.4 0.0 copy-done.2
  41.4 0.0 copy-done.3
  41.4 0.6 gate.1.refs_4_.refs_1_
  42.1 0.6 product_one.1
  42.7 0.3 collective-permute-done.refs_1_.refs_3_
  43.0 0.6 product_two.1
  43.6 17.2 %all_to_all.21 = bf16[128,4,128]{2,1,0:T(4,128)(2,1)S(1)} all-to-all(bf16[128,4,128]{2,1,0:T(4,128)(2,1)S(1)} %bitcast.34), channel_id=1, replica_groups=mesh['zl'=4,'co'=2,'y'=4,'x'=4,'zh'=2] {'zl','y','x','zh'}, dimensions={0} | all-to-all | bytes 262144 | tf_op jit(solution)/shard_map/all_to_all | solution.py:370
  60.8 0.2 tri_back.1
  61.0 16.7 %all_to_all.22 = bf16[128,4,128]{2,1,0:T(4,128)(2,1)S(1)} all-to-all(bf16[128,4,128]{2,1,0:T(4,128)(2,1)S(1)} %bitcast.33), channel_id=1, replica_groups=mesh['zl'=4,'co'=2,'y'=4,'x'=4,'zh'=2] {'zl','y','x','zh'}, dimensions={0} | all-to-all | bytes 262144 | tf_op jit(solution)/shard_map/all_to_all | solution.py:370
  77.7 2.7 %collective-permute-start.1 = (bf16[512,128]{1,0:T(8,128)(2,1)S(1)}, bf16[512,128]{1,0:T(8,128)(2,1)S(1)}, u32[]{:S(2)}, u32[]{:S(2)}) collective-permute-start(bf16[512,128]{1,0:T(8,128)(2,1)S(1)} %bitcast.27), channel_id=1, source_target_pairs={{0,32},{32,0},{1,33},{33,1},{2,34},{34,2},{3,35},{35,3},{4,36},{36... | collective-permute-start | bytes 393224 | tf_op jit(solution)/shard_map/ppermute | solution.py:374
  80.4 1.3 %product_three.1 = (f32[2304,128]{1,0:T(8,128)S(1)}, bf16[768,128]{1,0:T(8,128)(2,1)S(1)}) custom-call(s32[1]{0:T(128)} %bitcast.refs_0_, bf16[512,128]{1,0:T(8,128)(2,1)S(1)} %bitcast.28, bf16[768,128]{1,0:T(8,128)(2,1)S(1)} %get-tuple-element.15.refs_2_, bf16[2304,128]{1,0:T(8,128)(2,1)S(1)} %collective-permute-done.refs_1_.refs_3_, ...), custom_call_target="tpu_custom_call" | custom-call | flops 100000000 | bytes 2000000 | tf_op jit(solution)/shard_map/product_three/pallas_call | solution.py:355
  81.6 0.0 collective-permute-done.1.refs_1_
  81.7 1.3 %product_four.1 = bf16[2304,128]{1,0:T(8,128)(2,1)} custom-call(s32[1]{0:T(128)} %bitcast.refs_0_, bf16[512,128]{1,0:T(8,128)(2,1)S(1)} %collective-permute-done.1.refs_1_, bf16[768,128]{1,0:T(8,128)(2,1)S(1)} %get-tuple-element.21.refs_2_, f32[2304,128]{1,0:T(8,128)S(1)} %get-tuple-element.22.refs_3_), custom_call_target="tpu_custom_call" | custom-call | flops 100000000 | bytes 2000000 | tf_op jit(solution)/shard_map/product_four/pallas_call | solution.py:355
  83.0 6.4 %all-to-all-start.3 = ((bf16[128,9,2,128]{3,2,1,0:T(2,128)(2,1)}), bf16[128,9,2,128]{3,2,1,0:T(2,128)(2,1)S(1)}, u32[]{:S(2)}, u32[]{:S(2)}) async-start(bf16[128,9,2,128]{3,2,1,0:T(2,128)(2,1)} %bitcast.16), calls=%async_computation.3 | async-start | bytes 1179648 | tf_op jit(solution)/shard_map/all_to_all | solution.py:370
  89.3 2.6 %factors.1.refs_1_ = bf16[9728,128]{1,0:T(8,128)(2,1)S(1)} custom-call(f32[1,128]{1,0:T(1,128)} %bitcast.36, f32[1,128]{1,0:T(1,128)} %bitcast.40, bf16[128,256]{1,0:T(8,128)(2,1)} %refs_2_.3, bf16[768,128]{1,0:T(8,128)(2,1)} %bitcast.48, bf16[128,256]{1,0:T(8,128)(2,1)} %refs_4_.3, bf16[1536,128]{1,0:T(8,128)(2,1)} %bitcast.46), custom_call_target="tpu_custom_call" | custom-call | flops 100000000 | bytes 2000000 | tf_op jit(solution)/shard_map/factors/pallas_call | solution.py:355
  91.9 2.9 %tile.1 = (bf16[512,128]{1,0:T(8,128)(2,1)}, bf16[512,128]{1,0:T(8,128)(2,1)}) custom-call(bf16[512,128]{1,0:T(8,128)(2,1)S(1)} %bitcast.26, f32[1,128]{1,0:T(1,128)} %bitcast.37, f32[1,128]{1,0:T(1,128)} %bitcast.41, f32[1,128]{1,0:T(1,128)} %bitcast.43, f32[1,128]{1,0:T(1,128)} %bitcast.49, bf16[128,128]{1,0:T(8,128)(2,1)} %refs_5_.3, ...), custom_call_target="tpu_custom_call" | custom-call | flops 100000000 | bytes 2000000 | tf_op jit(solution)/shard_map/tile/pallas_call | solution.py:355
  94.8 14.3 %all-to-all-done.3 = bf16[128,9,2,128]{3,2,1,0:T(2,128)(2,1)S(1)} async-done(((bf16[128,9,2,128]{3,2,1,0:T(2,128)(2,1)}), bf16[128,9,2,128]{3,2,1,0:T(2,128)(2,1)S(1)}, u32[]{:S(2)}, u32[]{:S(2)}) %all-to-all-start.3) | async-done | bytes 589856 | tf_op jit(solution)/shard_map/all_to_all | solution.py:370
  109.2 1.8 %project_back.1 = (bf16[768,128]{1,0:T(8,128)(2,1)}, bf16[1536,128]{1,0:T(8,128)(2,1)}) custom-call(bf16[2304,128]{1,0:T(8,128)(2,1)S(1)} %bitcast.24, bf16[9728,128]{1,0:T(8,128)(2,1)S(1)} %factors.1.refs_1_), custom_call_target="tpu_custom_call" | custom-call | flops 100000000 | bytes 2000000 | tf_op jit(solution)/shard_map/project_back/pallas_call | solution.py:355
Async XLA Ops:
  0.6 40.8 %copy-start.4 = (f32[128]{0:T(128)S(1)}, f32[128]{0:T(128)}, u32[]{:S(2)}) copy-start(f32[128]{0:T(128)} %param.20) | copy-start | bytes 1540
  0.6 40.7 %copy-start.5 = (f32[128]{0:T(128)S(1)}, f32[128]{0:T(128)}, u32[]{:S(2)}) copy-start(f32[128]{0:T(128)} %param.21) | copy-start | bytes 1540
  0.7 40.7 %copy-start.6 = (f32[128]{0:T(128)S(1)}, f32[128]{0:T(128)}, u32[]{:S(2)}) copy-start(f32[128]{0:T(128)} %param.22) | copy-start | bytes 1540
  0.7 40.7 %copy-start = (bf16[32,16,128]{2,1,0:T(8,128)(2,1)S(1)}, bf16[32,16,128]{2,1,0:T(8,128)(2,1)}, u32[]{:S(2)}) copy-start(bf16[32,16,128]{2,1,0:T(8,128)(2,1)} %param.14) | copy-start | bytes 393220
  0.7 40.7 %copy-start.1 = (bf16[32,16,128]{2,1,0:T(8,128)(2,1)S(1)}, bf16[32,16,128]{2,1,0:T(8,128)(2,1)}, u32[]{:S(2)}) copy-start(bf16[32,16,128]{2,1,0:T(8,128)(2,1)} %param.15) | copy-start | bytes 393220
  0.7 40.7 %copy-start.2 = (bf16[128,128]{1,0:T(8,128)(2,1)S(1)}, bf16[128,128]{1,0:T(8,128)(2,1)}, u32[]{:S(2)}) copy-start(bf16[128,128]{1,0:T(8,128)(2,1)} %refs_5_.3) | copy-start | bytes 98308
  0.7 40.7 %copy-start.3 = (bf16[128,128]{1,0:T(8,128)(2,1)S(1)}, bf16[128,128]{1,0:T(8,128)(2,1)}, u32[]{:S(2)}) copy-start(bf16[128,128]{1,0:T(8,128)(2,1)} %refs_7_.1) | copy-start | bytes 98308
  38.4 4.6 %collective-permute-start = (bf16[2304,128]{1,0:T(8,128)(2,1)S(1)}, bf16[2304,128]{1,0:T(8,128)(2,1)S(1)}, u32[]{:S(2)}, u32[]{:S(2)}) collective-permute-start(bf16[2304,128]{1,0:T(8,128)(2,1)S(1)} %bitcast.21), channel_id=1, source_target_pairs={{0,32},{32,0},{1,33},{33,1},{2,34},{34,2},{3,35},{35,3},{4,36},{36... | collective-permute-start | bytes 1769480 | tf_op jit(solution)/shard_map/ppermute | solution.py:374
  77.7 4.0 %collective-permute-start.1 = (bf16[512,128]{1,0:T(8,128)(2,1)S(1)}, bf16[512,128]{1,0:T(8,128)(2,1)S(1)}, u32[]{:S(2)}, u32[]{:S(2)}) collective-permute-start(bf16[512,128]{1,0:T(8,128)(2,1)S(1)} %bitcast.27), channel_id=1, source_target_pairs={{0,32},{32,0},{1,33},{33,1},{2,34},{34,2},{3,35},{35,3},{4,36},{36... | collective-permute-start | bytes 393224 | tf_op jit(solution)/shard_map/ppermute | solution.py:374
  83.0 26.2 %all-to-all-start.3 = ((bf16[128,9,2,128]{3,2,1,0:T(2,128)(2,1)}), bf16[128,9,2,128]{3,2,1,0:T(2,128)(2,1)S(1)}, u32[]{:S(2)}, u32[]{:S(2)}) async-start(bf16[128,9,2,128]{3,2,1,0:T(2,128)(2,1)} %bitcast.16), calls=%async_computation.3 | async-start | bytes 1179648 | tf_op jit(solution)/shard_map/all_to_all | solution.py:370

commit v5 on v4

--- a/solution.py
+++ b/solution.py
@@ -270,7 +270,7 @@
                 sent[target, :] = base[target, :] + block[r * 32 : r * 32 + 32, :]
             else:
                 sent[target, :] = base[target, :]
-    out[...] = sent[...].astype(BF16)
+        out.put(zl * 32 * ROWS, sent[pl.ds(zl * 32 * ROWS, 32 * ROWS), :].astype(BF16))
 
 
 def edges_back(grad_edge, start, weights, kept):
@@ -302,8 +302,8 @@
             held.append(block[:96, :])
             if len(held) * 96 == SPAN:
                 start = (r + 1) * 96 - SPAN
-                grad_column[pl.ds(start, SPAN), :] = edges_back(
-                    jnp.concatenate(held, axis=0), 768 + start, w_right, kept
+                grad_column.put(
+                    start, edges_back(jnp.concatenate(held, axis=0), 768 + start, w_right, kept)
                 )
                 held = []
         else:
@@ -311,7 +311,7 @@
                 left_rows[pl.ds(tail_k(r, q), 32, stride=24), :] = block[q * 32 : q * 32 + 32, :]
     for step in range(768 // SPAN):
         rows = pl.ds(step * SPAN, SPAN)
-        grad_slab[rows, :] = edges_back(left_rows[rows, :], step * SPAN, w_left, kept)
+        grad_slab.put(step * SPAN, edges_back(left_rows[rows, :], step * SPAN, w_left, kept))
 
 
 VMEM = pl.BlockSpec(memory_space=pltpu.VMEM)
@@ -331,15 +331,36 @@
         return self.ref
 
 
-def run(kernel, name, outs, scratch, args, fetched=(), limit=16, cost=2_000_000):
-    cuts = [len(args), len(fetched), len(outs), len(scratch), len(fetched)]
+class Streamed:
+    def __init__(self, out, stage, sems, first):
+        self.out, self.stage, self.sems, self.at, self.copies = out, stage, sems, first, []
+
+    def put(self, start, value):
+        rows = pl.ds(start, value.shape[0])
+        self.stage[rows, :] = value
+        copy = pltpu.make_async_copy(
+            self.stage.at[rows, :], self.out.at[rows, :], self.sems.at[self.at]
+        )
+        copy.start()
+        self.at += 1
+        self.copies.append(copy)
+
+
+def run(kernel, name, outs, scratch, args, fetched=(), limit=16, cost=2_000_000, streamed=False):
+    staged_outs = outs if streamed else []
+    cuts = [len(args), len(fetched), len(outs), len(scratch), len(fetched), len(staged_outs)]
 
     def body(*refs):
         groups, at = [], 0
         for size in cuts:
             groups.append(refs[at : at + size])
             at += size
-        plain, sources, results, work, stages = groups
+        plain, sources, results, work, stages, out_stages = groups
+        if streamed:
+            results = [
+                Streamed(out, stage, refs[-1], 8 * n)
+                for n, (out, stage) in enumerate(zip(results, out_stages))
+            ]
         staged = [
             Staged(pltpu.make_async_copy(source, stage, refs[-1].at[n]), stage)
             for n, (source, stage) in enumerate(zip(sources, stages))
@@ -347,17 +368,24 @@
         kernel(*plain, *staged, *results, *work)
         for item in staged:
             item()
+        if streamed:
+            for result in results:
+                for copy in result.copies:
+                    copy.wait()
 
     scratches = [pltpu.VMEM((n, 128), F32) for n in scratch]
     scratches += [pltpu.VMEM(a.shape, a.dtype) for a in fetched]
+    scratches += [pltpu.VMEM(shape, dtype) for shape, dtype in staged_outs]
     if fetched:
         scratches.append(pltpu.SemaphoreType.DMA((len(fetched),)))
+    if streamed:
+        scratches.append(pltpu.SemaphoreType.DMA((8 * len(outs),)))
     return pl.pallas_call(
         body,
         name=name,
         out_shape=[jax.ShapeDtypeStruct(s, t) for s, t in outs],
         in_specs=[SMEM if a.dtype == jnp.int32 else VMEM for a in args] + [HBM] * len(fetched),
-        out_specs=[VMEM] * len(outs),
+        out_specs=[HBM if streamed else VMEM] * len(outs),
         scratch_shapes=scratches,
         cost_estimate=pl.CostEstimate(flops=50 * cost, bytes_accessed=cost, transcendentals=0),
         compiler_params=pltpu.CompilerParams(vmem_limit_bytes=limit and limit << 20),
@@ -430,7 +458,7 @@
     )
     (back_sent,) = run(
         fourth_product_kernel, "product_four", [((128 * ROWS, 128), BF16)],
-        [512, 512, 128 * ROWS], (core, d_come, left_come, base),
+        [512, 512, 128 * ROWS], (core, d_come, left_come, base), streamed=True,
     )
     back = shuffled(back_sent)
     (kept,) = run(
@@ -440,7 +468,7 @@
     )
     grad_slab, grad_column = run(
         project_back_kernel, "project_back",
-        [((768, 128), BF16), ((1536, 128), BF16)], [128 * ROWS, 768], (back, kept),
+        [((768, 128), BF16), ((1536, 128), BF16)], [128 * ROWS, 768], (back, kept), streamed=True,
     )
     return (
         update.reshape(pair_tile.shape),

time: 111 us -> 112 us (level)
  no operation moved by 1% of the time
where the time goes in v5:
time: 112 us; the launch traced here: 111 us
  blocking collectives  68.8 us (61%)
  waiting for transfers between devices  14.7 us (13%)
  Pallas kernels  14.6 us (13%)
  starting transfers between devices  12.1 us (11%)
    all_to_all x3, blocking collectives, shuffled(): lax.all_to_all(array.reshape(shape), SPLIT, 0, 0, tiled=True)  68.8 us
    pallas_call x10, Pallas kernels, run(): pl.pallas_call(body, name=name, out_shape=[jax.ShapeDtypeStruct(s, t) for...  14.6 us
    all_to_all x1, waiting for transfers between devices, shuffled(): lax.all_to_all(array.reshape(shape), SPLIT, 0, 0, tiled=True)  14.3 us
    all_to_all x1, starting transfers between devices, shuffled(): lax.all_to_all(array.reshape(shape), SPLIT, 0, 0, tiled=True)  6.37 us
    ppermute x2, starting transfers between devices, swapped(): return lax.ppermute(array, 'co', [(0, 1), (1, 0)])  5.71 us
  transfers between devices with their start and end apart: 3, of which 2 were waited for; matrix products, arithmetic and copies ran while one was open for 0% of the time, Pallas kernels for 7%

profile of v5, /device:TPU:1, one launch (start us, length us, event | category | flops | bytes accessed | tf_op | source)
XLA Modules:
  0.0 111.2 jit_solution(15561547185594149755)
XLA Ops:
  0.6 0.0 copy-start.4
  0.6 0.0 copy-start.5
  0.7 0.0 copy-start.6
  0.7 0.0 copy-start
  0.7 0.0 copy-start.1
  0.7 0.0 copy-start.2
  0.7 0.0 copy-start.3
  0.7 2.7 %project.1 = bf16[2304,128]{1,0:T(8,128)(2,1)S(1)} custom-call(f32[1,128]{1,0:T(1,128)} %bitcast.35, f32[1,128]{1,0:T(1,128)} %bitcast.39, bf16[128,256]{1,0:T(8,128)(2,1)} %refs_2_.3, bf16[768,128]{1,0:T(8,128)(2,1)} %bitcast.47, bf16[128,256]{1,0:T(8,128)(2,1)} %refs_4_.3, bf16[1536,128]{1,0:T(8,128)(2,1)} %bitcast.45), custom_call_target="tpu_custom_call" | custom-call | flops 100000000 | bytes 2000000 | tf_op jit(solution)/shard_map/project/pallas_call | solution.py:383
  3.4 35.0 %all_to_all.20 = bf16[128,9,2,128]{3,2,1,0:T(2,128)(2,1)S(1)} all-to-all(bf16[128,9,2,128]{3,2,1,0:T(2,128)(2,1)S(1)} %bitcast.23), channel_id=1, replica_groups=mesh['zl'=4,'co'=2,'y'=4,'x'=4,'zh'=2] {'zl','y','x','zh'}, dimensions={0} | all-to-all | bytes 1179648 | tf_op jit(solution)/shard_map/all_to_all | solution.py:398
  38.4 3.0 %collective-permute-start = (bf16[2304,128]{1,0:T(8,128)(2,1)S(1)}, bf16[2304,128]{1,0:T(8,128)(2,1)S(1)}, u32[]{:S(2)}, u32[]{:S(2)}) collective-permute-start(bf16[2304,128]{1,0:T(8,128)(2,1)S(1)} %bitcast.21), channel_id=1, source_target_pairs={{0,32},{32,0},{1,33},{33,1},{2,34},{34,2},{3,35},{35,3},{4,36},{36... | collective-permute-start | bytes 1769480 | tf_op jit(solution)/shard_map/ppermute | solution.py:402
  41.4 0.0 copy-done.4
  41.4 0.0 copy-done.5
  41.4 0.0 copy-done.6
  41.4 0.0 copy-done
  41.4 0.0 copy-done.1
  41.4 0.0 copy-done.2
  41.4 0.0 copy-done.3
  41.4 0.6 gate.1.refs_4_.refs_1_
  42.1 0.6 product_one.1
  42.7 0.3 collective-permute-done.refs_1_.refs_3_
  43.0 0.6 product_two.1
  43.6 17.2 %all_to_all.21 = bf16[128,4,128]{2,1,0:T(4,128)(2,1)S(1)} all-to-all(bf16[128,4,128]{2,1,0:T(4,128)(2,1)S(1)} %bitcast.34), channel_id=1, replica_groups=mesh['zl'=4,'co'=2,'y'=4,'x'=4,'zh'=2] {'zl','y','x','zh'}, dimensions={0} | all-to-all | bytes 262144 | tf_op jit(solution)/shard_map/all_to_all | solution.py:398
  60.8 0.2 tri_back.1
  61.0 16.7 %all_to_all.22 = bf16[128,4,128]{2,1,0:T(4,128)(2,1)S(1)} all-to-all(bf16[128,4,128]{2,1,0:T(4,128)(2,1)S(1)} %bitcast.33), channel_id=1, replica_groups=mesh['zl'=4,'co'=2,'y'=4,'x'=4,'zh'=2] {'zl','y','x','zh'}, dimensions={0} | all-to-all | bytes 262144 | tf_op jit(solution)/shard_map/all_to_all | solution.py:398
  77.7 2.7 %collective-permute-start.1 = (bf16[512,128]{1,0:T(8,128)(2,1)S(1)}, bf16[512,128]{1,0:T(8,128)(2,1)S(1)}, u32[]{:S(2)}, u32[]{:S(2)}) collective-permute-start(bf16[512,128]{1,0:T(8,128)(2,1)S(1)} %bitcast.27), channel_id=1, source_target_pairs={{0,32},{32,0},{1,33},{33,1},{2,34},{34,2},{3,35},{35,3},{4,36},{36... | collective-permute-start | bytes 393224 | tf_op jit(solution)/shard_map/ppermute | solution.py:402
  80.4 1.3 %product_three.1 = (f32[2304,128]{1,0:T(8,128)S(1)}, bf16[768,128]{1,0:T(8,128)(2,1)S(1)}) custom-call(s32[1]{0:T(128)} %bitcast.refs_0_, bf16[512,128]{1,0:T(8,128)(2,1)S(1)} %bitcast.28, bf16[768,128]{1,0:T(8,128)(2,1)S(1)} %get-tuple-element.15.refs_2_, bf16[2304,128]{1,0:T(8,128)(2,1)S(1)} %collective-permute-done.refs_1_.refs_3_, ...), custom_call_target="tpu_custom_call" | custom-call | flops 100000000 | bytes 2000000 | tf_op jit(solution)/shard_map/product_three/pallas_call | solution.py:383
  81.6 0.0 collective-permute-done.1.refs_1_
  81.7 1.3 %product_four.1 = bf16[2304,128]{1,0:T(8,128)(2,1)} custom-call(s32[1]{0:T(128)} %bitcast.refs_0_, bf16[512,128]{1,0:T(8,128)(2,1)S(1)} %collective-permute-done.1.refs_1_, bf16[768,128]{1,0:T(8,128)(2,1)S(1)} %get-tuple-element.21.refs_2_, f32[2304,128]{1,0:T(8,128)S(1)} %get-tuple-element.22.refs_3_), custom_call_target="tpu_custom_call" | custom-call | flops 100000000 | bytes 2000000 | tf_op jit(solution)/shard_map/product_four/pallas_call | solution.py:383
  83.0 6.4 %all-to-all-start.3 = ((bf16[128,9,2,128]{3,2,1,0:T(2,128)(2,1)}), bf16[128,9,2,128]{3,2,1,0:T(2,128)(2,1)S(1)}, u32[]{:S(2)}, u32[]{:S(2)}) async-start(bf16[128,9,2,128]{3,2,1,0:T(2,128)(2,1)} %bitcast.16), calls=%async_computation.3 | async-start | bytes 1179648 | tf_op jit(solution)/shard_map/all_to_all | solution.py:398
  89.3 2.6 %factors.1.refs_1_ = bf16[9728,128]{1,0:T(8,128)(2,1)S(1)} custom-call(f32[1,128]{1,0:T(1,128)} %bitcast.36, f32[1,128]{1,0:T(1,128)} %bitcast.40, bf16[128,256]{1,0:T(8,128)(2,1)} %refs_2_.3, bf16[768,128]{1,0:T(8,128)(2,1)} %bitcast.48, bf16[128,256]{1,0:T(8,128)(2,1)} %refs_4_.3, bf16[1536,128]{1,0:T(8,128)(2,1)} %bitcast.46), custom_call_target="tpu_custom_call" | custom-call | flops 100000000 | bytes 2000000 | tf_op jit(solution)/shard_map/factors/pallas_call | solution.py:383
  91.9 2.9 %tile.1 = (bf16[512,128]{1,0:T(8,128)(2,1)}, bf16[512,128]{1,0:T(8,128)(2,1)}) custom-call(bf16[512,128]{1,0:T(8,128)(2,1)S(1)} %bitcast.26, f32[1,128]{1,0:T(1,128)} %bitcast.37, f32[1,128]{1,0:T(1,128)} %bitcast.41, f32[1,128]{1,0:T(1,128)} %bitcast.43, f32[1,128]{1,0:T(1,128)} %bitcast.49, bf16[128,128]{1,0:T(8,128)(2,1)} %refs_5_.3, ...), custom_call_target="tpu_custom_call" | custom-call | flops 100000000 | bytes 2000000 | tf_op jit(solution)/shard_map/tile/pallas_call | solution.py:383
  94.8 14.3 %all-to-all-done.3 = bf16[128,9,2,128]{3,2,1,0:T(2,128)(2,1)S(1)} async-done(((bf16[128,9,2,128]{3,2,1,0:T(2,128)(2,1)}), bf16[128,9,2,128]{3,2,1,0:T(2,128)(2,1)S(1)}, u32[]{:S(2)}, u32[]{:S(2)}) %all-to-all-start.3) | async-done | bytes 589856 | tf_op jit(solution)/shard_map/all_to_all | solution.py:398
  109.2 1.9 %project_back.1 = (bf16[768,128]{1,0:T(8,128)(2,1)}, bf16[1536,128]{1,0:T(8,128)(2,1)}) custom-call(bf16[2304,128]{1,0:T(8,128)(2,1)S(1)} %bitcast.24, bf16[9728,128]{1,0:T(8,128)(2,1)S(1)} %factors.1.refs_1_), custom_call_target="tpu_custom_call" | custom-call | flops 100000000 | bytes 2000000 | tf_op jit(solution)/shard_map/project_back/pallas_call | solution.py:383
Async XLA Ops:
  0.6 40.8 %copy-start.4 = (f32[128]{0:T(128)S(1)}, f32[128]{0:T(128)}, u32[]{:S(2)}) copy-start(f32[128]{0:T(128)} %param.20) | copy-start | bytes 1540
  0.6 40.7 %copy-start.5 = (f32[128]{0:T(128)S(1)}, f32[128]{0:T(128)}, u32[]{:S(2)}) copy-start(f32[128]{0:T(128)} %param.21) | copy-start | bytes 1540
  0.7 40.7 %copy-start.6 = (f32[128]{0:T(128)S(1)}, f32[128]{0:T(128)}, u32[]{:S(2)}) copy-start(f32[128]{0:T(128)} %param.22) | copy-start | bytes 1540
  0.7 40.7 %copy-start = (bf16[32,16,128]{2,1,0:T(8,128)(2,1)S(1)}, bf16[32,16,128]{2,1,0:T(8,128)(2,1)}, u32[]{:S(2)}) copy-start(bf16[32,16,128]{2,1,0:T(8,128)(2,1)} %param.14) | copy-start | bytes 393220
  0.7 40.7 %copy-start.1 = (bf16[32,16,128]{2,1,0:T(8,128)(2,1)S(1)}, bf16[32,16,128]{2,1,0:T(8,128)(2,1)}, u32[]{:S(2)}) copy-start(bf16[32,16,128]{2,1,0:T(8,128)(2,1)} %param.15) | copy-start | bytes 393220
  0.7 40.7 %copy-start.2 = (bf16[128,128]{1,0:T(8,128)(2,1)S(1)}, bf16[128,128]{1,0:T(8,128)(2,1)}, u32[]{:S(2)}) copy-start(bf16[128,128]{1,0:T(8,128)(2,1)} %refs_5_.3) | copy-start | bytes 98308
  0.7 40.7 %copy-start.3 = (bf16[128,128]{1,0:T(8,128)(2,1)S(1)}, bf16[128,128]{1,0:T(8,128)(2,1)}, u32[]{:S(2)}) copy-start(bf16[128,128]{1,0:T(8,128)(2,1)} %refs_7_.1) | copy-start | bytes 98308
  38.4 4.6 %collective-permute-start = (bf16[2304,128]{1,0:T(8,128)(2,1)S(1)}, bf16[2304,128]{1,0:T(8,128)(2,1)S(1)}, u32[]{:S(2)}, u32[]{:S(2)}) collective-permute-start(bf16[2304,128]{1,0:T(8,128)(2,1)S(1)} %bitcast.21), channel_id=1, source_target_pairs={{0,32},{32,0},{1,33},{33,1},{2,34},{34,2},{3,35},{35,3},{4,36},{36... | collective-permute-start | bytes 1769480 | tf_op jit(solution)/shard_map/ppermute | solution.py:402
  77.7 4.0 %collective-permute-start.1 = (bf16[512,128]{1,0:T(8,128)(2,1)S(1)}, bf16[512,128]{1,0:T(8,128)(2,1)S(1)}, u32[]{:S(2)}, u32[]{:S(2)}) collective-permute-start(bf16[512,128]{1,0:T(8,128)(2,1)S(1)} %bitcast.27), channel_id=1, source_target_pairs={{0,32},{32,0},{1,33},{33,1},{2,34},{34,2},{3,35},{35,3},{4,36},{36... | collective-permute-start | bytes 393224 | tf_op jit(solution)/shard_map/ppermute | solution.py:402
  83.0 26.2 %all-to-all-start.3 = ((bf16[128,9,2,128]{3,2,1,0:T(2,128)(2,1)}), bf16[128,9,2,128]{3,2,1,0:T(2,128)(2,1)S(1)}, u32[]{:S(2)}, u32[]{:S(2)}) async-start(bf16[128,9,2,128]{3,2,1,0:T(2,128)(2,1)} %bitcast.16), calls=%async_computation.3 | async-start | bytes 1179648 | tf_op jit(solution)/shard_map/all_to_all | solution.py:398
